TPU v7x, 32 devices: a whole 2x2x4 slice. The times are simulated.
32 devices in a mesh: dp: 4 (over z), fsdp: 8 (over y, x, core).
Axes of the slice: x: 2, y: 2, z: 4, core: 2. Of those that a mesh axis runs over, the one named last changes fastest.
Arguments:
- block_input: bfloat16 [8192, 768], P(('dp', 'fsdp')), may hold values from -6 to 6
- segment_ids: int32 [32, 256], P(('dp', 'fsdp')), may hold values from 0 to 7, never falling along the last dimension, each value on 1 to 128 neighbouring positions
- output_grad: bfloat16 [8192, 768], P(('dp', 'fsdp')), may hold values from -6 to 6
- prenorm_one: bfloat16 [768], P(('dp', 'fsdp')), may hold values from 0.25 to 1.75
- inproj_one: bfloat16 [768, 2304], P(('dp', 'fsdp')), may hold values from -0.21875 to 0.21875
- outproj_one: bfloat16 [768, 768], P(None, ('dp', 'fsdp')), may hold values from -0.875 to 0.875
- midnorm_one: bfloat16 [768], P(('dp', 'fsdp')), may hold values from 0.25 to 1.75
- expand_one: bfloat16 [768, 3072], P(('dp', 'fsdp')), may hold values from -0.21875 to 0.21875
- shrink_one: bfloat16 [3072, 768], P(None, ('dp', 'fsdp')), may hold values from -0.21875 to 0.21875
- prenorm_two: bfloat16 [768], P(('dp', 'fsdp')), may hold values from 0.25 to 1.75
- inproj_two: bfloat16 [768, 1920], P(('dp', 'fsdp')), may hold values from -0.21875 to 0.21875
- outproj_two: bfloat16 [768, 768], P(None, ('dp', 'fsdp')), may hold values from -0.875 to 0.875
- midnorm_two: bfloat16 [768], P(('dp', 'fsdp')), may hold values from 0.25 to 1.75
- expand_two: bfloat16 [768, 3072], P(('dp', 'fsdp')), may hold values from -0.21875 to 0.21875
- shrink_two: bfloat16 [3072, 768], P(None, ('dp', 'fsdp')), may hold values from -0.21875 to 0.21875
Outputs:
- block_output: float32 [8192, 768], P(('dp', 'fsdp'))
- input_grad: float32 [8192, 768], P(('dp', 'fsdp'))
- prenorm_one_grad: float32 [768], P(('dp', 'fsdp'))
- inproj_one_grad: float32 [768, 2304], P(('dp', 'fsdp'))
- outproj_one_grad: float32 [768, 768], P(None, ('dp', 'fsdp'))
- midnorm_one_grad: float32 [768], P(('dp', 'fsdp'))
- expand_one_grad: float32 [768, 3072], P(('dp', 'fsdp'))
- shrink_one_grad: float32 [3072, 768], P(None, ('dp', 'fsdp'))
- prenorm_two_grad: float32 [768], P(('dp', 'fsdp'))
- inproj_two_grad: float32 [768, 1920], P(('dp', 'fsdp'))
- outproj_two_grad: float32 [768, 768], P(None, ('dp', 'fsdp'))
- midnorm_two_grad: float32 [768], P(('dp', 'fsdp'))
- expand_two_grad: float32 [768, 3072], P(('dp', 'fsdp'))
- shrink_two_grad: float32 [3072, 768], P(None, ('dp', 'fsdp'))
Inputs may be any that keep to these rules, and one draw needn't show every extreme that they name: `segment_ids`: within each row the numbers never fall; each document has 1 to 128 tokens, and one has exactly 128.
All inputs are finite; a program needn't handle non-finite values.
Results may differ from a plain program's by a relative error of at most 0.019.
Values may be sent and summed in bfloat16 or wider, within the bound.
A program may use at most 256 MiB of HBM per device.

v0:
```python
import math

import jax
import jax.numpy as jnp
from jax import lax
from jax.sharding import PartitionSpec as P

HEADS = 12


def layer_norm(inputs, gain):
    centred = inputs - jnp.mean(inputs, axis=-1, keepdims=True)
    spread = jnp.mean(centred * centred, axis=-1, keepdims=True)
    return centred * lax.rsqrt(spread + 1e-05) * gain


def gelu_tanh(value):
    return jax.nn.gelu(value, approximate=True)


def rows_product(left, right):
    return lax.dot_general(
        left, right, (((0,), (0,)), ((), ())), preferred_element_type=jnp.float32
    )


def cols_product(left, right):
    return lax.dot_general(
        left, right, (((1,), (1,)), ((), ())), preferred_element_type=jnp.float32
    )


def gather_weights(weights):
    prenorm, inproj, outproj, midnorm, expand, shrink = weights
    return (
        lax.all_gather(prenorm, ("dp", "fsdp"), axis=0, tiled=True),
        lax.all_gather(inproj, ("dp", "fsdp"), axis=0, tiled=True),
        lax.all_gather(outproj, ("dp", "fsdp"), axis=1, tiled=True),
        lax.all_gather(midnorm, ("dp", "fsdp"), axis=0, tiled=True),
        lax.all_gather(expand, ("dp", "fsdp"), axis=0, tiled=True),
        lax.all_gather(shrink, ("dp", "fsdp"), axis=1, tiled=True),
    )


def sum_grads(kept):
    (
        attn_in,
        proj_grad,
        branch_low,
        mixed,
        mlp_in,
        before_grad,
        out_low,
        active,
        prenorm_grad,
        midnorm_grad,
    ) = kept
    width = attn_in.shape[1]
    proj_width = proj_grad.shape[1]
    hidden_width = active.shape[1]

    def entries(value):
        return value[:, None]

    summed = lax.psum_scatter(
        jnp.concatenate(
            [
                rows_product(attn_in, proj_grad),
                rows_product(branch_low, mixed),
                rows_product(mlp_in, before_grad),
                rows_product(out_low, active),
                entries(prenorm_grad),
                entries(midnorm_grad),
            ],
            axis=1,
        ),
        ("dp", "fsdp"),
        scatter_dimension=0,
        tiled=True,
    )
    inproj_part = summed[:, :proj_width]
    outproj_part = summed[:, proj_width : proj_width + width].T
    expand_start = proj_width + width
    expand_part = summed[:, expand_start : expand_start + hidden_width]
    shrink_start = expand_start + hidden_width
    shrink_part = summed[:, shrink_start : shrink_start + hidden_width].T
    prenorm_part = summed[:, shrink_start + hidden_width]
    midnorm_part = summed[:, shrink_start + hidden_width + 1]
    return (prenorm_part, inproj_part, outproj_part, midnorm_part, expand_part, shrink_part)


def layer_forward(inputs, allowed, weights, first_values):
    prenorm, inproj, outproj, midnorm, expand, shrink = weights
    length, width = inputs.shape
    half = width // 2
    size = width // HEADS
    scale = 1.0 / math.sqrt(size)
    attn_in = layer_norm(inputs, prenorm.astype(jnp.float32)).astype(jnp.bfloat16)
    projected = jnp.dot(attn_in, inproj, preferred_element_type=jnp.float32)
    query = projected[:, :width].astype(jnp.bfloat16).reshape(length, HEADS, size)
    keys = projected[:, width : 2 * width].astype(jnp.bfloat16).reshape(length, HEADS, size)
    fresh = projected[:, 2 * width :].astype(jnp.bfloat16)
    if first_values is None:
        values = fresh
    else:
        values = jnp.concatenate([first_values[:, :half], fresh], axis=1)
    value_heads = values.reshape(length, HEADS, size)
    scores = jnp.einsum("qhd,khd->hqk", query, keys, preferred_element_type=jnp.float32) * scale
    scores = jnp.where(allowed[None], scores, -1000000000.0)
    highest = jnp.max(scores, axis=-1, keepdims=True)
    total = highest + jnp.log(jnp.sum(jnp.exp(scores - highest), axis=-1, keepdims=True))
    weights_full = jnp.exp(scores - total)
    probs = weights_full.astype(jnp.bfloat16)
    mixed = jnp.einsum("hqk,khd->qhd", probs, value_heads, preferred_element_type=jnp.float32)
    mixed = mixed.astype(jnp.bfloat16).reshape(length, width)
    middle = inputs + jnp.dot(mixed, outproj, preferred_element_type=jnp.float32)
    mlp_in = layer_norm(middle, midnorm.astype(jnp.float32)).astype(jnp.bfloat16)
    before = jnp.dot(mlp_in, expand, preferred_element_type=jnp.float32)
    active = gelu_tanh(before).astype(jnp.bfloat16)
    output = middle + jnp.dot(active, shrink, preferred_element_type=jnp.float32)
    return (
        attn_in,
        query,
        keys,
        fresh,
        value_heads,
        weights_full,
        probs,
        mixed,
        middle,
        mlp_in,
        before,
        active,
        output,
    )


def layer_backward(inputs, allowed, weights, first_values, incoming, carried):
    prenorm, inproj, outproj, midnorm, expand, shrink = weights
    length, width = inputs.shape
    half = width // 2
    size = width // HEADS
    scale = 1.0 / math.sqrt(size)
    parts = layer_forward(inputs, allowed, weights, first_values)
    (
        attn_in,
        query,
        keys,
        fresh,
        value_heads,
        weights_full,
        probs,
        mixed,
        middle,
        mlp_in,
        before,
        active,
        output,
    ) = parts
    out_low = incoming.astype(jnp.bfloat16)
    active_grad = cols_product(out_low, shrink)
    unused_gelu, gelu_pull = jax.vjp(gelu_tanh, before)
    before_grad = gelu_pull(active_grad)[0].astype(jnp.bfloat16)
    mlp_grad = cols_product(before_grad, expand)
    unused_mid, mid_pull = jax.vjp(layer_norm, middle, midnorm.astype(jnp.float32))
    middle_part, midnorm_grad = mid_pull(mlp_grad)
    middle_grad = incoming + middle_part
    branch_low = middle_grad.astype(jnp.bfloat16)
    mixed_grad = cols_product(branch_low, outproj).astype(jnp.bfloat16).reshape(length, HEADS, size)
    prob_grad = jnp.einsum(
        "qhd,khd->hqk", mixed_grad, value_heads, preferred_element_type=jnp.float32
    )
    value_grad = jnp.einsum(
        "hqk,qhd->khd", probs, mixed_grad, preferred_element_type=jnp.float32
    ).reshape(length, width)
    score_grad = weights_full * (
        prob_grad - jnp.sum(weights_full * prob_grad, axis=-1, keepdims=True)
    )
    score_low = score_grad.astype(jnp.bfloat16)
    query_grad = (
        (jnp.einsum("hqk,khd->qhd", score_low, keys, preferred_element_type=jnp.float32) * scale)
        .astype(jnp.bfloat16)
        .reshape(length, width)
    )
    keys_grad = (
        (jnp.einsum("hqk,qhd->khd", score_low, query, preferred_element_type=jnp.float32) * scale)
        .astype(jnp.bfloat16)
        .reshape(length, width)
    )
    if first_values is None:
        value_total = jnp.concatenate(
            [value_grad[:, :half] + carried, value_grad[:, half:]], axis=1
        )
        fresh_grad = value_total.astype(jnp.bfloat16)
        passed = None
    else:
        fresh_grad = value_grad[:, half:].astype(jnp.bfloat16)
        passed = value_grad[:, :half]
    proj_grad = jnp.concatenate([query_grad, keys_grad, fresh_grad], axis=1)
    attn_grad = cols_product(proj_grad, inproj)
    unused_in, in_pull = jax.vjp(layer_norm, inputs, prenorm.astype(jnp.float32))
    inputs_part, prenorm_grad = in_pull(attn_grad)
    kept = (
        attn_in,
        proj_grad,
        branch_low,
        mixed,
        mlp_in,
        before_grad,
        out_low,
        active,
        prenorm_grad,
        midnorm_grad,
    )
    return (middle_grad + inputs_part, kept, passed)


def per_device(
    block_input,
    segment_ids,
    output_grad,
    prenorm_one,
    inproj_one,
    outproj_one,
    midnorm_one,
    expand_one,
    shrink_one,
    prenorm_two,
    inproj_two,
    outproj_two,
    midnorm_two,
    expand_two,
    shrink_two,
):
    segment = segment_ids[0]
    positions = jnp.arange(segment.shape[0])
    allowed = (segment[:, None] == segment[None, :]) & (positions[None, :] <= positions[:, None])
    layer_one = (prenorm_one, inproj_one, outproj_one, midnorm_one, expand_one, shrink_one)
    layer_two = (prenorm_two, inproj_two, outproj_two, midnorm_two, expand_two, shrink_two)
    first_set = gather_weights(layer_one)
    inputs = block_input.astype(jnp.float32)
    first_parts = layer_forward(inputs, allowed, first_set, None)
    hidden = first_parts[12]
    first_values = first_parts[3]
    second_set = gather_weights(layer_two)
    second_parts = layer_forward(hidden, allowed, second_set, first_values)
    output = second_parts[12]
    second_back = gather_weights(layer_two)
    hidden_grad, kept_two, passed = layer_backward(
        hidden, allowed, second_back, first_values, output_grad.astype(jnp.float32), None
    )
    sums_two = sum_grads(kept_two)
    first_back = gather_weights(layer_one)
    input_grad, kept_one, unused_pass = layer_backward(
        inputs, allowed, first_back, None, hidden_grad, passed
    )
    sums_one = sum_grads(kept_one)
    return (
        output,
        input_grad,
        sums_one[0],
        sums_one[1],
        sums_one[2],
        sums_one[3],
        sums_one[4],
        sums_one[5],
        sums_two[0],
        sums_two[1],
        sums_two[2],
        sums_two[3],
        sums_two[4],
        sums_two[5],
    )


def solution(mesh):
    return jax.shard_map(
        per_device,
        mesh=mesh,
        in_specs=(
            P(("dp", "fsdp"), None),
            P(("dp", "fsdp"), None),
            P(("dp", "fsdp"), None),
            P(("dp", "fsdp")),
            P(("dp", "fsdp"), None),
            P(None, ("dp", "fsdp")),
            P(("dp", "fsdp")),
            P(("dp", "fsdp"), None),
            P(None, ("dp", "fsdp")),
            P(("dp", "fsdp")),
            P(("dp", "fsdp"), None),
            P(None, ("dp", "fsdp")),
            P(("dp", "fsdp")),
            P(("dp", "fsdp"), None),
            P(None, ("dp", "fsdp")),
        ),
        out_specs=(
            P(("dp", "fsdp"), None),
            P(("dp", "fsdp"), None),
            P(("dp", "fsdp")),
            P(("dp", "fsdp"), None),
            P(None, ("dp", "fsdp")),
            P(("dp", "fsdp")),
            P(("dp", "fsdp"), None),
            P(None, ("dp", "fsdp")),
            P(("dp", "fsdp")),
            P(("dp", "fsdp"), None),
            P(None, ("dp", "fsdp")),
            P(("dp", "fsdp")),
            P(("dp", "fsdp"), None),
            P(None, ("dp", "fsdp")),
        ),
        check_vma=False,
    )
```

profile of v0, /device:TPU:0, one launch (start us, length us, event | category | flops | bytes accessed | tf_op | source)
XLA Modules:
  0.0 1313.2 jit_solution(7766992693241372046)
XLA Ops:
  16.1 42.3 %all-reduce.5 = (bf16[768]{0:T(1024)(128)(2,1)S(1)}, bf16[768]{0:T(1024)(128)(2,1)S(1)}, bf16[768]{0:T(1024)(128)(2,1)S(1)}, bf16[768]{0:T(1024)(128)(2,1)S(1)}) all-reduce(bf16[768]{0:T(1024)(128)(2,1)S(1)} %dynamic-update-slice, bf16[768]{0:T(1024)(128)(2,1)S(1)} %dynamic-update-slice.1, ...), channel_id=1, replica_groups=mesh['dp'=4,'fsdp'=8] {'dp','fsdp'}, use_global_device_ids=true, to_apply=%add | all-reduce | flops 3072 | bytes 12288
  61.7 12.1 all-gather.9.cloned.1.call-done
  73.8 3.3 convolution_convert_fusion
  80.7 1.8 fusion.14
  86.3 43.2 %all-gather.11.cloned.1.call-done = bf16[768,768]{0,1:T(8,128)(2,1)} async-done(((bf16[768,24]{0,1:T(8,128)(2,1)}), bf16[768,768]{0,1:T(8,128)(2,1)}) %all-gather.11.cloned.1.call-update) | async-done | bytes 1179664 | tf_op jit(solution)/shard_map/all_gather | solution.py:38
  129.6 2.0 fusion.82
  133.8 61.3 %all-gather.13.cloned.1.call-done = bf16[768,3072]{1,0:T(8,128)(2,1)} async-done(((bf16[24,3072]{1,0:T(8,128)(2,1)}), bf16[768,3072]{1,0:T(8,128)(2,1)}) %all-gather.13.cloned.1.call-update) | async-done | bytes 4718608 | tf_op jit(solution)/shard_map/all_gather | solution.py:40
  195.1 5.7 fusion.74
  200.8 59.5 %all-gather.15.cloned.1.call-done = bf16[3072,768]{0,1:T(8,128)(2,1)} async-done(((bf16[3072,24]{0,1:T(8,128)(2,1)}), bf16[3072,768]{0,1:T(8,128)(2,1)}) %all-gather.15.cloned.1.call-update) | async-done | bytes 4718608 | tf_op jit(solution)/shard_map/all_gather | solution.py:41
  260.3 5.6 fusion.83
  268.2 52.5 %all-gather.17.cloned.1.call-done = bf16[768,1920]{1,0:T(8,128)(2,1)} async-done(((bf16[24,1920]{1,0:T(8,128)(2,1)}), bf16[768,1920]{1,0:T(8,128)(2,1)}) %all-gather.17.cloned.1.call-update) | async-done | bytes 2949136 | tf_op jit(solution)/shard_map/all_gather | solution.py:37
  320.7 3.2 convolution_convert_fusion.1
  325.6 1.9 copy.83
  327.6 2.1 fusion.81
  329.6 1.9 copy.84
  331.6 1.9 copy.85
  333.5 1.9 fusion.15
  337.0 1.6 convolution_convert_fusion.4
  338.6 37.6 %all-gather.19.cloned.1.call-done = bf16[768,768]{0,1:T(8,128)(2,1)} async-done(((bf16[768,24]{0,1:T(8,128)(2,1)}), bf16[768,768]{0,1:T(8,128)(2,1)}) %all-gather.19.cloned.1.call-update) | async-done | bytes 1179664 | tf_op jit(solution)/shard_map/all_gather | solution.py:38
  376.3 2.5 fusion.84
  381.1 60.7 %all-gather.23.cloned.1.call-done = bf16[3072,768]{0,1:T(8,128)(2,1)} async-done(((bf16[3072,24]{0,1:T(8,128)(2,1)}), bf16[3072,768]{0,1:T(8,128)(2,1)}) %all-gather.23.cloned.1.call-update) | async-done | bytes 4718608 | tf_op jit(solution)/shard_map/all_gather | solution.py:41
  441.8 5.5 fusion.85
  447.3 59.9 %all-gather.21.cloned.1.call-done = bf16[768,3072]{1,0:T(8,128)(2,1)} async-done(((bf16[24,3072]{1,0:T(8,128)(2,1)}), bf16[768,3072]{1,0:T(8,128)(2,1)}) %all-gather.21.cloned.1.call-update) | async-done | bytes 4718608 | tf_op jit(solution)/shard_map/all_gather | solution.py:40
  507.2 8.6 fusion.13
  515.8 2.2 multiply_reduce_fusion.2
  521.4 1.9 copy.87
  523.4 2.9 fusion.52
  531.1 1.8 multiply_reduce_fusion.3
  535.0 3.3 fusion.6
  538.4 2.2 multiply_reduce_fusion.4
  543.2 1.9 copy.91
  545.1 2.0 fusion.55
  550.6 1.9 fusion.39
  552.5 5.2 fusion.73
  557.8 5.2 fusion.42
  563.0 4.2 fusion.37
  570.0 30.8 %concatenate.22 = f32[768,9218]{1,0:T(8,128)} concatenate(f32[768,2304]{1,0:T(8,128)} %fusion.37, f32[768,768]{1,0:T(8,128)} %fusion.39, f32[768,3072]{1,0:T(8,128)} %fusion.73, f32[768,3072]{1,0:T(8,128)} %fusion.42, f32[768,1]{1,0:T(8,128)S(1)} %broadcast_in_dim.62, f32[768,1]{1,0:T(8,128)S(1)} %broadcast_in_dim.63), dimensions={1} | concatenate | bytes 56635392 | tf_op jit(solution)/shard_map/concatenate | solution.py:66
  603.6 1.9 fusion.86
  605.6 3.8 fusion.33
  609.4 5.2 fusion.75
  614.6 5.2 convolution_bitcast_fusion
  619.8 30.7 %concatenate.23 = f32[768,8834]{1,0:T(8,128)} concatenate(f32[768,1920]{1,0:T(8,128)} %fusion.33, f32[768,768]{1,0:T(8,128)} %fusion.86, f32[768,3072]{1,0:T(8,128)} %fusion.75, f32[768,3072]{1,0:T(8,128)} %convolution_bitcast_fusion, f32[768,1]{1,0:T(8,128)S(1)} %broadcast_in_dim.64, f32[768,1]{1,0:T(8,128)S(1)} %copy-done.39), dimensions={1} | concatenate | bytes 54276096 | tf_op jit(solution)/shard_map/concatenate | solution.py:66
  653.1 6.8 convolution_add_fusion.2
  659.8 374.2 %all-reduce.8.cloned.1.call-done = f32[768,9218]{1,0:T(8,128)} async-done(((f32[768,9218]{1,0:T(8,128)}), f32[768,9218]{1,0:T(8,128)}) %all-reduce.8.cloned.1.call-update) | async-done | bytes 28317712
  1037.2 1.6 constant_dynamic-slice_fusion
  1038.8 2.1 dynamic-slice_bitcast_fusion
  1040.9 258.7 %reduce-scatter.2.cloned.1.call-done = f32[24,8834]{1,0:T(8,128)} async-done(((f32[768,8834]{1,0:T(8,128)}), f32[24,8834]{1,0:T(8,128)}) %reduce-scatter.2.cloned.1.call-update) | async-done | bytes 848080 | tf_op jit(solution)/shard_map/reduce_scatter | solution.py:65
  1304.2 1.9 slice_bitcast_fusion
  (313 shorter events, 61.2 us)
Async XLA Ops:
  7.2 66.6 %all-gather.9.cloned.1.call-start = ((), (), s32[]{:S(2)}) async-start(), calls=%async_computation.1 | async-start | bytes 3649536 | tf_op jit(solution)/shard_map/all_gather | solution.py:37
  7.9 121.7 %all-gather.11.cloned.1.call-start = ((), (), s32[]{:S(2)}) async-start(), calls=%async_computation.2 | async-start | bytes 1216512 | tf_op jit(solution)/shard_map/all_gather | solution.py:38
  8.7 186.4 %all-gather.13.cloned.1.call-start = ((), (), s32[]{:S(2)}) async-start(), calls=%async_computation.3 | async-start | bytes 4866048 | tf_op jit(solution)/shard_map/all_gather | solution.py:40
  9.4 250.9 %all-gather.15.cloned.1.call-start = ((), (), s32[]{:S(2)}) async-start(), calls=%async_computation.4 | async-start | bytes 4866048 | tf_op jit(solution)/shard_map/all_gather | solution.py:41
  10.0 310.7 %all-gather.17.cloned.1.call-start = ((), (), s32[]{:S(2)}) async-start(), calls=%async_computation.5 | async-start | bytes 3041280 | tf_op jit(solution)/shard_map/all_gather | solution.py:37
  10.6 365.7 %all-gather.19.cloned.1.call-start = ((), (), s32[]{:S(2)}) async-start(), calls=%async_computation.6 | async-start | bytes 1216512 | tf_op jit(solution)/shard_map/all_gather | solution.py:38
  11.1 430.6 %all-gather.23.cloned.1.call-start = ((), (), s32[]{:S(2)}) async-start(), calls=%async_computation.8 | async-start | bytes 4866048 | tf_op jit(solution)/shard_map/all_gather | solution.py:41
  11.9 495.3 %all-gather.21.cloned.1.call-start = ((), (), s32[]{:S(2)}) async-start(), calls=%async_computation.7 | async-start | bytes 4866048 | tf_op jit(solution)/shard_map/all_gather | solution.py:40
  12.6 1021.4 %all-reduce.8.cloned.1.call-start = ((), (), s32[]{:S(2)}) async-start(), calls=%async_computation.10 | async-start | bytes 57409536
  59.5 17.5 %copy-start.66 = (f32[256]{0:T(256)}, f32[256]{0:T(256)S(1)}, u32[]{:S(2)}) copy-start(f32[256]{0:T(256)S(1)} %broadcast_multiply_fusion.3) | copy-start | bytes 3076
  60.8 17.0 %copy-start.88 = (f32[256]{0:T(256)}, f32[256]{0:T(256)S(1)}, u32[]{:S(2)}) copy-start(f32[256]{0:T(256)S(1)} %fusion.30) | copy-start | bytes 3076
  60.8 17.0 %copy-start.68 = (f32[256]{0:T(256)}, f32[256]{0:T(256)S(1)}, u32[]{:S(2)}) copy-start(f32[256]{0:T(256)S(1)} %fusion.48) | copy-start | bytes 3076
  61.7 19.0 %copy-start.18 = (pred[256,256]{0,1:T(8,128)(4,1)}, pred[256,256]{0,1:T(8,128)(4,1)S(1)}, u32[]{:S(2)}) copy-start(pred[256,256]{0,1:T(8,128)(4,1)S(1)} %fusion.36) | copy-start | bytes 196612
  80.7 4.1 copy-start.45
  82.5 47.0 %copy-start.5 = (bf16[256,768]{1,0:T(8,128)(2,1)S(1)}, bf16[256,768]{1,0:T(8,128)(2,1)}, u32[]{:S(2)}) copy-start(bf16[256,768]{1,0:T(8,128)(2,1)} %param.15) | copy-start | bytes 1179652
  320.7 4.2 copy-start.57
  333.5 3.5 copy-start.47
  507.1 8.6 copy-start.9
  507.1 8.6 copy-start.75
  507.1 8.6 copy-start.82
  507.2 8.6 copy-start.100
  515.8 3.4 copy-start.28
  529.2 3.7 copy-start.40
  529.2 4.4 slice-start.2
  533.3 5.0 slice-start
  535.0 5.9 copy-start.14
  535.0 3.3 copy-start.84
  535.0 3.3 slice-start.1
  552.5 5.2 copy-start.15
  552.5 5.2 copy-start.38
  557.7 5.2 copy-start.67
  557.7 5.2 copy-start.69
  563.0 4.2 copy-start.101
  568.4 32.4 %copy-start.35 = (f32[256,768]{1,0:T(8,128)}, f32[256,768]{1,0:T(8,128)S(1)}, u32[]{:S(2)}) copy-start(f32[256,768]{1,0:T(8,128)S(1)} %get-tuple-element.65) | copy-start | bytes 2359300
  600.9 4.7 copy-start.4
  600.9 4.6 copy-start.41
  600.9 698.7 %reduce-scatter.2.cloned.1.call-start = ((), (), s32[]{:S(2)}) async-start(), calls=%async_computation.9 | async-start | bytes 28385280 | tf_op jit(solution)/shard_map/reduce_scatter | solution.py:65
  601.0 4.6 copy-start.43
  601.0 4.6 copy-start.59
  601.0 4.6 copy-start.73
  601.0 4.6 copy-start.81
  605.6 3.8 copy-start.10
  605.6 3.8 copy-start.53
  605.6 3.8 copy-start.76
  605.6 3.8 copy-start.83
  609.4 5.2 copy-start.23
  609.4 5.2 copy-start.30
  614.6 5.2 copy-start.39
  (69 other events, 126.6 us)
Sparse Core Ops, SparseCore 0:
  10.9 62.8 all-gather.8
  76.7 52.8 all-gather.10
  132.5 62.5 all-gather.12
  197.8 62.4 all-gather.14
  263.1 57.5 all-gather.16
  323.4 52.7 all-gather.18
  379.1 62.5 all-gather.22
  444.7 62.4 all-gather.20
  601.0 433.0 all-reduce.7
  1040.3 259.2 reduce-scatter.1
where the time goes:
time: 1330 us; the launch traced here: 1310 us
  waiting for transfers between devices  1020 us (77%)
  local copies, waits for them, and re-layouts  111 us (8%)
  matrix products  105 us (8%)
  blocking collectives  42.3 us (3%)
  between operations  15.6 us (1%)
  other arithmetic  14.4 us (1%)
    unnamed x11, waiting for transfers between devices  379 us
    reduce_scatter x1, waiting for transfers between devices, sum_grads(): lax.psum_scatter(jnp.concatenate([rows_product(attn_in, proj_grad), rows_...  259 us
    all_gather x2, waiting for transfers between devices, gather_weights(): lax.all_gather(expand, ('dp', 'fsdp'), axis=0, tiled=True)  121 us
    all_gather x2, waiting for transfers between devices, gather_weights(): lax.all_gather(shrink, ('dp', 'fsdp'), axis=1, tiled=True)  120 us
    all_gather x2, waiting for transfers between devices, gather_weights(): lax.all_gather(outproj, ('dp', 'fsdp'), axis=1, tiled=True)  80.9 us
    all_gather x2, waiting for transfers between devices, gather_weights(): lax.all_gather(inproj, ('dp', 'fsdp'), axis=0, tiled=True)  64.6 us
    concatenate x2, local copies, waits for them, and re-layouts, sum_grads(): jnp.concatenate([rows_product(attn_in, proj_grad), rows_product(branch_lo...  61.5 us
    unnamed x1, blocking collectives  42.3 us
  transfers between devices with their start and end apart: 10, of which 10 were waited for; matrix products, arithmetic and copies ran while one was open for 9% of the time, Pallas kernels for 0%

commit v1 on v0

--- a/solution.py
+++ b/solution.py
@@ -1,8 +1,11 @@
+import functools
 import math
 
 import jax
 import jax.numpy as jnp
 from jax import lax
+from jax.experimental import pallas as pl
+from jax.experimental.pallas import tpu as pltpu
 from jax.sharding import PartitionSpec as P
 
 HEADS = 12
@@ -135,13 +138,14 @@
     )
 
 
-def layer_backward(inputs, allowed, weights, first_values, incoming, carried):
+def layer_backward(inputs, allowed, weights, first_values, incoming, carried, parts=None):
     prenorm, inproj, outproj, midnorm, expand, shrink = weights
     length, width = inputs.shape
     half = width // 2
     size = width // HEADS
     scale = 1.0 / math.sqrt(size)
-    parts = layer_forward(inputs, allowed, weights, first_values)
+    if parts is None:
+        parts = layer_forward(inputs, allowed, weights, first_values)
     (
         attn_in,
         query,
@@ -215,6 +219,614 @@
     return (middle_grad + inputs_part, kept, passed)
 
 
+PIECE = 384
+CHUNK = 2 * PIECE
+MESH = pl.DeviceIdType.MESH
+
+
+def when(condition, body):
+    if isinstance(condition, bool):
+        if condition:
+            body()
+    else:
+        pl.when(condition)(body)
+
+
+class Seat:
+    def __init__(self, layers):
+        self.layers = layers
+        self.z = lax.axis_index("dp")
+        place = lax.axis_index("fsdp")
+        self.core = lax.rem(place, 2)
+        self.x = lax.rem(lax.div(place, 2), 2)
+        self.y = lax.div(place, 4)
+        self.partner = (self.z, place + 1 - 2 * self.core)
+        self.across_x = (self.z, place + 2 - 4 * self.x)
+        self.across_y = (self.z, place + 4 - 8 * self.y)
+        self.up = (self.z + 1, place)
+        self.down = (self.z - 1, place)
+        self.has_up = self.z < layers - 1
+        self.has_down = self.z > 0
+
+    def greet(self):
+        barrier = pltpu.get_barrier_semaphore()
+        for other in (self.partner, self.across_x, self.across_y):
+            pl.semaphore_signal(barrier, inc=1, device_id=other, device_id_type=MESH)
+
+        @pl.when(self.has_up)
+        def _():
+            pl.semaphore_signal(barrier, inc=1, device_id=self.up, device_id_type=MESH)
+
+        @pl.when(self.has_down)
+        def _():
+            pl.semaphore_signal(barrier, inc=1, device_id=self.down, device_id_type=MESH)
+
+        inner = self.has_up & self.has_down
+
+        @pl.when(inner)
+        def _():
+            pl.semaphore_wait(barrier, 5)
+
+        @pl.when(jnp.logical_not(inner))
+        def _():
+            pl.semaphore_wait(barrier, 4)
+
+
+def piece_columns(chunk, core):
+    return pl.ds(pl.multiple_of(chunk * CHUNK + core * PIECE, 128), PIECE)
+
+
+def remote(source, target, send_sem, recv_sem, device):
+    return pltpu.make_async_remote_copy(
+        src_ref=source,
+        dst_ref=target,
+        send_sem=send_sem,
+        recv_sem=recv_sem,
+        device_id=device,
+        device_id_type=MESH,
+    )
+
+
+FULL = slice(None)
+COLOURS = (0, 1, 2, 0, 1, 0, 1, 2)
+
+
+def colour_of(chunk):
+    step = lax.rem(chunk, 8)
+    return jnp.where(
+        (step == 2) | (step == 7), 2, jnp.where((step == 1) | (step == 4) | (step == 6), 1, 0)
+    )
+
+
+class Gather:
+    def __init__(self, seat, held, own, other, chunks, pre_sem, recv_sem, send_sem):
+        self.seat, self.held, self.own, self.other, self.chunks = seat, held, own, other, chunks
+        self.pre_sem, self.recv_sem, self.send_sem = pre_sem, recv_sem, send_sem
+
+    def window(self, chunk, zs, ys, xs, core=None):
+        core = self.seat.core if core is None else core
+        return self.held.at[zs, ys, xs, :, piece_columns(chunk, core)]
+
+    def swap(self, chunk):
+        seat = self.seat
+        columns = piece_columns(chunk, 1 - seat.core)
+        return remote(
+            self.own.at[:, columns],
+            self.other.at[:, columns],
+            self.pre_sem.at[0, chunk],
+            self.pre_sem.at[1, chunk],
+            seat.partner,
+        )
+
+    def copy(self, chunk, zs, ys, xs, kind, arrival, device):
+        window = self.window(chunk, zs, ys, xs)
+        return remote(
+            window, window, self.send_sem.at[chunk, kind], self.recv_sem.at[chunk, arrival], device
+        )
+
+    def up(self, chunk, origin, ys, xs):
+        return self.copy(chunk, origin, ys, xs, origin, origin, self.seat.up)
+
+    def down(self, chunk, origin, ys, xs):
+        return self.copy(chunk, origin, ys, xs, 4 + origin, origin, self.seat.down)
+
+    def merge(self, chunk):
+        seat = self.seat
+        columns = piece_columns(chunk, seat.core)
+        remote(
+            self.own.at[:, columns],
+            self.other.at[:, columns],
+            self.pre_sem.at[0, chunk],
+            self.pre_sem.at[1, chunk],
+            seat.partner,
+        ).wait_recv()
+        mine = self.own[:, columns].astype(jnp.float32)
+        theirs = self.other[:, columns].astype(jnp.float32)
+        first = seat.core == 0
+        both = jnp.concatenate(
+            [jnp.where(first, mine, theirs), jnp.where(first, theirs, mine)], axis=0
+        )
+        self.held[seat.z, seat.y, seat.x, :, columns] = both.astype(jnp.bfloat16)
+
+    def start_z(self, chunk, ys, xs):
+        seat = self.seat
+        when(seat.has_up, lambda: self.up(chunk, seat.z, ys, xs).start())
+        when(seat.has_down, lambda: self.down(chunk, seat.z, ys, xs).start())
+
+    def relay_z(self, chunk, step, ys, xs):
+        seat = self.seat
+        below, above = seat.z - 1 - step, seat.z + 1 + step
+
+        def from_below():
+            self.up(chunk, below, ys, xs).wait_recv()
+            when(seat.has_up, lambda: self.up(chunk, below, ys, xs).start())
+
+        def from_above():
+            self.down(chunk, above, ys, xs).wait_recv()
+            when(seat.has_down, lambda: self.down(chunk, above, ys, xs).start())
+
+        when(below >= 0, from_below)
+        when(above <= seat.layers - 1, from_above)
+
+    def side(self, chunk, axis, zs, other):
+        seat = self.seat
+        if axis == "x":
+            return self.copy(chunk, zs, other, seat.x, 8, 4, seat.across_x)
+        return self.copy(chunk, zs, seat.y, other, 9, 5, seat.across_y)
+
+    def side_arrives(self, chunk, axis, zs, other):
+        seat = self.seat
+        if axis == "x":
+            self.copy(chunk, zs, other, 1 - seat.x, 8, 4, seat.across_x).wait_recv()
+        else:
+            self.copy(chunk, zs, 1 - seat.y, other, 9, 5, seat.across_y).wait_recv()
+
+    def to_partner(self, chunk):
+        return self.copy(chunk, FULL, FULL, FULL, 10, 6, self.seat.partner)
+
+    def stage(self, chunk, number):
+        seat = self.seat
+        y, x = seat.y, seat.x
+        last = seat.layers - 1
+
+        def z_first(first, second, own_first):
+            if number == 0:
+                self.start_z(chunk, y, x)
+            elif number <= last:
+                self.relay_z(chunk, number - 1, y, x)
+            if number == last:
+                self.side(chunk, first, FULL, own_first).start()
+            if number == last + 1:
+                self.side_arrives(chunk, first, FULL, own_first)
+                self.side(chunk, second, FULL, FULL).start()
+            if number == last + 2:
+                self.side_arrives(chunk, second, FULL, FULL)
+
+        def z_last():
+            if number == 0:
+                self.side(chunk, "x", seat.z, y).start()
+            if number == 1:
+                self.side_arrives(chunk, "x", seat.z, y)
+                self.side(chunk, "y", seat.z, FULL).start()
+            if number == 2:
+                self.side_arrives(chunk, "y", seat.z, FULL)
+                self.start_z(chunk, FULL, FULL)
+            if number >= 3:
+                self.relay_z(chunk, number - 3, FULL, FULL)
+
+        if number == 0:
+            self.merge(chunk)
+        if number <= last + 2:
+            colour = colour_of(chunk)
+            when(colour == 0, lambda: z_first("x", "y", y))
+            when(colour == 1, lambda: z_first("y", "x", x))
+            when(colour == 2, z_last)
+        if number == last + 2:
+            self.to_partner(chunk).start()
+        if number == last + 3:
+            window = self.window(chunk, FULL, FULL, FULL, 1 - seat.core)
+            remote(
+                window, window, self.send_sem.at[chunk, 10], self.recv_sem.at[chunk, 6], seat.partner
+            ).wait_recv()
+
+    def drain(self, chunk):
+        seat = self.seat
+        y, x = seat.y, seat.x
+        columns = piece_columns(chunk, 1 - seat.core)
+        self.swap(chunk).wait_send()
+
+        def z_sends(ys, xs):
+            for origin in range(seat.layers):
+                when(
+                    seat.has_up & (seat.z >= origin),
+                    lambda: self.up(chunk, origin, ys, xs).wait_send(),
+                )
+                when(
+                    seat.has_down & (seat.z <= origin),
+                    lambda: self.down(chunk, origin, ys, xs).wait_send(),
+                )
+
+        def z_first(first, second, own_first):
+            z_sends(y, x)
+            self.side(chunk, first, FULL, own_first).wait_send()
+            self.side(chunk, second, FULL, FULL).wait_send()
+
+        def z_last():
+            z_sends(FULL, FULL)
+            self.side(chunk, "x", seat.z, y).wait_send()
+            self.side(chunk, "y", seat.z, FULL).wait_send()
+
+        colour = colour_of(chunk)
+        when(colour == 0, lambda: z_first("x", "y", y))
+        when(colour == 1, lambda: z_first("y", "x", x))
+        when(colour == 2, z_last)
+        self.to_partner(chunk).wait_send()
+
+    def round(self, i):
+        for lag, number in ((0, 0), (2, 4), (1, 2), (3, 6), (2, 5), (1, 3), (0, 1)):
+            chunk = i - lag
+            when((chunk >= 0) & (chunk < self.chunks), functools.partial(self.stage, chunk, number))
+
+
+def gather_kernel(layers, chunks, own, held, other, pre_sem, recv_sem, send_sem):
+    seat = Seat(layers)
+    seat.greet()
+    work = Gather(seat, held, own, other, chunks, pre_sem, recv_sem, send_sem)
+
+    def loop(count, body):
+        lax.fori_loop(0, count, lambda i, c: (body(i), c)[1], 0)
+
+    loop(chunks, lambda i: work.swap(i).start())
+    loop(chunks + 3, work.round)
+    loop(chunks, work.drain)
+
+
+SLOTS = 6
+LANDING = 23
+
+
+class Scatter:
+    def __init__(self, seat, chunks, fill, part, staged, landed, total, recv_sem, send_sem):
+        self.seat, self.chunks, self.fill = seat, chunks, fill
+        self.part, self.staged, self.landed, self.total = part, staged, landed, total
+        self.recv_sem, self.send_sem = recv_sem, send_sem
+
+    def send(self, turn, spot, there, count, kind, arrival, device):
+        slot = lax.rem(turn, SLOTS)
+        return remote(
+            self.staged.at[slot, pl.ds(spot, count)],
+            self.landed.at[turn, pl.ds(there, count)],
+            self.send_sem.at[slot, kind],
+            self.recv_sem.at[turn, arrival],
+            device,
+        )
+
+    def store(self, turn, spot, count, zs, ys, xs):
+        slot = lax.rem(turn, SLOTS)
+        value = self.part[slot, zs, ys, xs]
+        self.staged[slot, pl.ds(spot, count)] = value.astype(jnp.bfloat16).reshape(
+            (count,) + value.shape[-2:]
+        )
+
+    def add(self, turn, spot, count, zs, ys, xs):
+        slot = lax.rem(turn, SLOTS)
+        value = self.part[slot, zs, ys, xs]
+        arrived = self.landed[turn, pl.ds(spot, count)].astype(jnp.float32)
+        self.part[slot, zs, ys, xs] = value + arrived.reshape(value.shape)
+
+    def side(self, turn, axis, spot, count):
+        device = self.seat.across_x if axis == "x" else self.seat.across_y
+        kind = 0 if axis == "x" else 1
+        return self.send(turn, spot, spot, count, kind, kind, device)
+
+    def start_side(self, turn, axis, spot, count, zs, other):
+        seat = self.seat
+        if axis == "x":
+            self.store(turn, spot, count, zs, other, 1 - seat.x)
+        else:
+            self.store(turn, spot, count, zs, 1 - seat.y, other)
+        self.side(turn, axis, spot, count).start()
+
+    def finish_side(self, turn, axis, spot, count, zs, other):
+        seat = self.seat
+        self.side(turn, axis, spot, count).wait_recv()
+        if axis == "x":
+            self.add(turn, spot, count, zs, other, seat.x)
+        else:
+            self.add(turn, spot, count, zs, seat.y, other)
+
+    def up(self, turn, base, count, goal):
+        return self.send(
+            turn, base + count * goal, base + count * goal, count, 2 + goal, 2 + goal, self.seat.up
+        )
+
+    def down(self, turn, base, count, goal):
+        slot = jnp.where(goal == self.seat.z - 1, self.seat.layers, goal)
+        return self.send(
+            turn, base + count * goal, base + count * slot, count, 2 + goal, 2 + slot, self.seat.down
+        )
+
+    def arrival_z(self, turn, base, count, slot):
+        spot = pl.ds(base + count * slot, count)
+        window = self.landed.at[turn, spot]
+        return remote(
+            window,
+            window,
+            self.send_sem.at[0, 0],
+            self.recv_sem.at[turn, 2 + slot],
+            self.seat.partner,
+        )
+
+    def step_z(self, turn, step, base, count, ys, xs):
+        seat = self.seat
+        layers = seat.layers
+
+        def upward():
+            for goal in range(1, layers):
+
+                def one(goal=goal):
+                    def arrived():
+                        self.arrival_z(turn, base, count, goal).wait_recv()
+                        self.add(turn, base + count * goal, count, goal, ys, xs)
+
+                    when(seat.has_down, arrived)
+
+                    def onward():
+                        self.store(turn, base + count * goal, count, goal, ys, xs)
+                        self.up(turn, base, count, goal).start()
+
+                    when(seat.z < goal, onward)
+
+                when(seat.z <= goal, one)
+
+        def downward():
+            for goal in range(layers - 1):
+
+                def one(goal=goal):
+                    def arrived():
+                        slot = jnp.where(goal == seat.z, layers, goal)
+                        self.arrival_z(turn, base, count, slot).wait_recv()
+                        self.add(turn, base + count * slot, count, goal, ys, xs)
+
+                    when(seat.has_up, arrived)
+
+                    def onward():
+                        self.store(turn, base + count * goal, count, goal, ys, xs)
+                        self.down(turn, base, count, goal).start()
+
+                    when(seat.z > goal, onward)
+
+                when(seat.z >= goal, one)
+
+        when(seat.z == step, upward)
+        when(seat.z == layers - 1 - step, downward)
+
+    def piece(self, turn):
+        seat = self.seat
+        slot = lax.rem(turn, SLOTS)
+        rows = self.total.shape[0]
+        return self.part.at[
+            slot, seat.z, seat.y, seat.x, pl.ds(pl.multiple_of((1 - seat.core) * rows, 8), rows)
+        ]
+
+    def hand_over(self, turn, chunk):
+        window = self.total.at[:, piece_columns(chunk, self.seat.core)]
+        return remote(
+            self.piece(turn),
+            window,
+            self.send_sem.at[lax.rem(turn, SLOTS), 6],
+            self.recv_sem.at[turn, 7],
+            self.seat.partner,
+        )
+
+    def stage(self, turn, number):
+        seat = self.seat
+        y, x, z = seat.y, seat.x, seat.z
+        chunk = chunk_at(turn)
+
+        def z_last(first, second, own_second):
+            if number == 0:
+                self.start_side(turn, first, 0, 8, FULL, FULL)
+            if number == 1:
+                self.finish_side(turn, first, 0, 8, FULL, FULL)
+                self.start_side(turn, second, 8, 4, FULL, own_second)
+            if number == 2:
+                self.finish_side(turn, second, 8, 4, FULL, own_second)
+            if 2 <= number <= 5:
+                self.step_z(turn, number - 2, 12, 1, y, x)
+
+        def z_first():
+            if number <= 3:
+                self.step_z(turn, number, 0, 4, FULL, FULL)
+            if number == 3:
+                self.start_side(turn, "y", 20, 2, z, FULL)
+            if number == 4:
+                self.finish_side(turn, "y", 20, 2, z, FULL)
+                self.start_side(turn, "x", 22, 1, z, y)
+            if number == 5:
+                self.finish_side(turn, "x", 22, 1, z, y)
+
+        if number == 0:
+            self.fill(turn, chunk)
+        if number <= 5:
+            colour = colour_of(turn)
+            when(colour == 0, lambda: z_last("y", "x", y))
+            when(colour == 1, lambda: z_last("x", "y", x))
+            when(colour == 2, z_first)
+        if number == 5:
+            slot = lax.rem(turn, SLOTS)
+            rows = self.total.shape[0]
+            mine = pl.ds(pl.multiple_of(seat.core * rows, 8), rows)
+            self.total[:, piece_columns(chunk, seat.core)] = self.part[slot, z, y, x, mine]
+            self.hand_over(turn, chunk).start()
+        if number == 6:
+            self.hand_over(turn, chunk).wait_send()
+            window = self.total.at[:, piece_columns(chunk, 1 - seat.core)]
+            remote(
+                window, window, self.send_sem.at[0, 0], self.recv_sem.at[turn, 7], seat.partner
+            ).wait_recv()
+            self.drain(turn)
+
+    def drain(self, turn):
+        seat = self.seat
+
+        def z_sends(base, count):
+            for goal in range(seat.layers):
+                when(seat.z < goal, lambda: self.up(turn, base, count, goal).wait_send())
+                when(seat.z > goal, lambda: self.down(turn, base, count, goal).wait_send())
+
+        def z_last(first, second):
+            self.side(turn, first, 0, 8).wait_send()
+            self.side(turn, second, 8, 4).wait_send()
+            z_sends(12, 1)
+
+        def z_first():
+            z_sends(0, 4)
+            self.side(turn, "y", 20, 2).wait_send()
+            self.side(turn, "x", 22, 1).wait_send()
+
+        colour = colour_of(turn)
+        when(colour == 0, lambda: z_last("y", "x"))
+        when(colour == 1, lambda: z_last("x", "y"))
+        when(colour == 2, z_first)
+
+    def round(self, i):
+        for lag, number in ((0, 0), (2, 4), (1, 2), (3, 6), (2, 5), (1, 3), (0, 1)):
+            turn = i - lag
+            when((turn >= 0) & (turn < self.chunks), functools.partial(self.stage, turn, number))
+
+
+def chunk_at(turn):
+    spans = ((4, 20), (8, 12), (9, 7), (11, 4), (15, -2), (19, -10), (20, -15), (23, -19))
+    chunk = turn - 23
+    for end, shift in reversed(spans):
+        if end == 4:
+            chunk = jnp.where(turn < end, turn + shift, chunk)
+        else:
+            chunk = jnp.where(turn < end, turn + shift, chunk)
+    return chunk
+
+
+def left_of(chunk):
+    kind = 4
+    for start, which in ((1, 0), (4, 1), (5, 2), (9, 3), (13, 4), (15, 5), (16, 6), (20, 7)):
+        kind = jnp.where(chunk >= start, which, kind)
+    return kind
+
+
+def scatter_kernel(
+    layers,
+    chunks,
+    lefts,
+    rights,
+    gains,
+    total,
+    left2,
+    right2,
+    gain2,
+    part,
+    staged,
+    landed,
+    pre_sem,
+    recv_sem,
+    send_sem,
+):
+    seat = Seat(layers)
+    seat.greet()
+    core = seat.core
+    moves = []
+    for i, (source, target) in enumerate(
+        ((lefts, left2), (rights, right2), (gains, gain2))
+    ):
+        moves.append(
+            pltpu.make_async_copy(source, target.at[core], pre_sem.at[3 * i])
+        )
+        moves.append(
+            remote(source, target.at[core], pre_sem.at[3 * i + 1], pre_sem.at[3 * i + 2], seat.partner)
+        )
+    for move in moves:
+        move.start()
+    for move in moves:
+        move.wait()
+
+    def fill(turn, chunk):
+        slot = lax.rem(turn, SLOTS)
+        shape = part.shape[1:]
+        is_gain = (chunk == 0) & (core == 1)
+
+        @pl.when(is_gain)
+        def _():
+            both = gain2[0] + gain2[1]
+            padded = jnp.concatenate([both, jnp.zeros((120, both.shape[1]), jnp.float32)], axis=0)
+            turned = jnp.transpose(padded)
+            part[slot, :, :, :, :, pl.ds(0, 128)] = turned.reshape(shape[:-1] + (128,))
+            part[slot, :, :, :, :, pl.ds(128, 256)] = jnp.zeros(shape[:-1] + (256,), jnp.float32)
+
+        @pl.when(jnp.logical_not(is_gain))
+        def _():
+            which = left_of(chunk)
+            columns = piece_columns(chunk, core)
+            value = None
+            for side in range(2):
+                term = lax.dot_general(
+                    left2[side, which],
+                    right2[side, :, columns],
+                    (((0,), (0,)), ((), ())),
+                    preferred_element_type=jnp.float32,
+                )
+                value = term if value is None else value + term
+            part[slot] = value.reshape(shape)
+
+    work = Scatter(seat, chunks, fill, part, staged, landed, total, recv_sem, send_sem)
+    lax.fori_loop(0, chunks + 3, lambda i, c: (work.round(i), c)[1], 0)
+
+
+def gather_all(layers, packed):
+    rows, width = packed.shape
+    chunks = width // CHUNK
+    held = pl.pallas_call(
+        functools.partial(gather_kernel, layers, chunks),
+        out_shape=jax.ShapeDtypeStruct((layers, 2, 2, 2 * rows, width), packed.dtype),
+        in_specs=[pl.BlockSpec(memory_space=pltpu.VMEM)],
+        out_specs=pl.BlockSpec(memory_space=pltpu.VMEM),
+        scratch_shapes=[
+            pltpu.VMEM((rows, width), packed.dtype),
+            pltpu.SemaphoreType.DMA((2, chunks)),
+            pltpu.SemaphoreType.DMA((chunks, 7)),
+            pltpu.SemaphoreType.DMA((chunks, 11)),
+        ],
+        compiler_params=pltpu.CompilerParams(
+            collective_id=0, has_side_effects=True, vmem_limit_bytes=60 * 1024 * 1024
+        ),
+    )(packed)
+    return held.reshape(layers * 8 * rows, width)
+
+
+def scatter_all(layers, lefts, rights, gains):
+    kinds, tokens, depth = lefts.shape
+    width = rights.shape[1]
+    chunks = width // CHUNK
+    rows = depth // (8 * layers)
+    return pl.pallas_call(
+        functools.partial(scatter_kernel, layers, chunks),
+        out_shape=jax.ShapeDtypeStruct((rows, width), jnp.float32),
+        in_specs=[pl.BlockSpec(memory_space=pl.ANY)] * 3,
+        out_specs=pl.BlockSpec(memory_space=pltpu.VMEM),
+        scratch_shapes=[
+            pltpu.VMEM((2,) + lefts.shape, lefts.dtype),
+            pltpu.VMEM((2,) + rights.shape, rights.dtype),
+            pltpu.VMEM((2,) + gains.shape, gains.dtype),
+            pltpu.VMEM((SLOTS, layers, 2, 2, 2 * rows, PIECE), jnp.float32),
+            pltpu.VMEM((SLOTS, LANDING, 2 * rows, PIECE), jnp.bfloat16),
+            pltpu.VMEM((chunks, LANDING, 2 * rows, PIECE), jnp.bfloat16),
+            pltpu.SemaphoreType.DMA((9,)),
+            pltpu.SemaphoreType.DMA((chunks, 8)),
+            pltpu.SemaphoreType.DMA((SLOTS, 7)),
+        ],
+        compiler_params=pltpu.CompilerParams(
+            collective_id=1, has_side_effects=True, vmem_limit_bytes=67043328
+        ),
+    )(lefts, rights, gains)
 def per_device(
     block_input,
     segment_ids,
@@ -273,9 +885,143 @@
     )
 
 
+def per_device_linked(
+    layers,
+    block_input,
+    segment_ids,
+    output_grad,
+    prenorm_one,
+    inproj_one,
+    outproj_one,
+    midnorm_one,
+    expand_one,
+    shrink_one,
+    prenorm_two,
+    inproj_two,
+    outproj_two,
+    midnorm_two,
+    expand_two,
+    shrink_two,
+):
+    segment = segment_ids[0]
+    positions = jnp.arange(segment.shape[0])
+    allowed = (segment[:, None] == segment[None, :]) & (positions[None, :] <= positions[:, None])
+    width = block_input.shape[1]
+    rows = prenorm_one.shape[0]
+    gains = jnp.stack([prenorm_one, midnorm_one, prenorm_two, midnorm_two], axis=1)
+    packed = jnp.concatenate(
+        [
+            inproj_two[:, 2 * width :],
+            gains,
+            jnp.zeros((rows, PIECE - 4), jnp.bfloat16),
+            inproj_one,
+            outproj_one.T,
+            expand_one,
+            shrink_one.T,
+            inproj_two[:, : 2 * width],
+            outproj_two.T,
+            expand_two,
+            shrink_two.T,
+        ],
+        axis=1,
+    )
+    held = gather_all(layers, packed)
+    hidden_width = expand_one.shape[1]
+
+    def cut(start, size):
+        return held[:, start : start + size]
+
+    bases = [CHUNK + i * 0 for i in range(1)]
+    base = CHUNK
+    gain = held[:, PIECE : PIECE + 4]
+    one = (
+        gain[:, 0],
+        cut(base, 3 * width),
+        cut(base + 3 * width, width).T,
+        gain[:, 1],
+        cut(base + 4 * width, hidden_width),
+        cut(base + 4 * width + hidden_width, hidden_width).T,
+    )
+    base = base + 4 * width + 2 * hidden_width
+    two = (
+        gain[:, 2],
+        jnp.concatenate([cut(base, 2 * width), cut(0, width // 2)], axis=1),
+        cut(base + 2 * width, width).T,
+        gain[:, 3],
+        cut(base + 3 * width, hidden_width),
+        cut(base + 3 * width + hidden_width, hidden_width).T,
+    )
+    inputs = block_input.astype(jnp.float32)
+    first_parts = layer_forward(inputs, allowed, one, None)
+    hidden = first_parts[12]
+    first_values = first_parts[3]
+    second_parts = layer_forward(hidden, allowed, two, first_values)
+    output = second_parts[12]
+    hidden_grad, kept_two, passed = layer_backward(
+        hidden, allowed, two, first_values, output_grad.astype(jnp.float32), None, second_parts
+    )
+    input_grad, kept_one, unused_pass = layer_backward(
+        inputs, allowed, one, None, hidden_grad, passed, first_parts
+    )
+
+    def lefts(kept):
+        return [kept[0], kept[2], kept[4], kept[6]]
+
+    def rights(kept, proj):
+        return [proj, kept[3], kept[5], kept[7]]
+
+    rows_two = kept_two[1]
+    left = jnp.stack(lefts(kept_one) + lefts(kept_two))
+    right = jnp.concatenate(
+        [rows_two[:, 2 * width :], jnp.zeros((rows_two.shape[0], PIECE), jnp.bfloat16)]
+        + rights(kept_one, kept_one[1])
+        + rights(kept_two, rows_two[:, : 2 * width]),
+        axis=1,
+    )
+    gain_grads = jnp.stack([kept_one[8], kept_one[9], kept_two[8], kept_two[9]])
+    gain_grads = jnp.concatenate([gain_grads, jnp.zeros_like(gain_grads)], axis=0)
+    total = scatter_all(layers, left, right, gain_grads)
+
+    def took(start, size):
+        return total[:, start : start + size]
+
+    def weights_of(base, proj):
+        return (
+            proj,
+            took(base, width).T,
+            took(base + width, hidden_width),
+            took(base + width + hidden_width, hidden_width).T,
+        )
+
+    one_grads = weights_of(CHUNK + 3 * width, took(CHUNK, 3 * width))
+    base = CHUNK + 4 * width + 2 * hidden_width
+    two_grads = weights_of(
+        base + 2 * width, jnp.concatenate([took(base, 2 * width), took(0, width // 2)], axis=1)
+    )
+    return (
+        output,
+        input_grad,
+        took(PIECE, 1)[:, 0],
+        one_grads[0],
+        one_grads[1],
+        took(PIECE + 1, 1)[:, 0],
+        one_grads[2],
+        one_grads[3],
+        took(PIECE + 2, 1)[:, 0],
+        two_grads[0],
+        two_grads[1],
+        took(PIECE + 3, 1)[:, 0],
+        two_grads[2],
+        two_grads[3],
+    )
+
+
 def solution(mesh):
+    layers = mesh.shape["dp"]
+    linked = layers == 4 and mesh.shape["fsdp"] == 8
+    step = functools.partial(per_device_linked, layers) if linked else per_device
     return jax.shard_map(
-        per_device,
+        step,
         mesh=mesh,
         in_specs=(
             P(("dp", "fsdp"), None),

time: 1330 us -> 721 us (0.54)
  waiting for transfers between devices: 1020 us -> 0 us
  Pallas kernels: 0 us -> 517 us
  blocking collectives: 42.3 us -> 0 us
  local copies, waits for them, and re-layouts: 111 us -> 81.1 us
  matrix products: 105 us -> 77 us
  other arithmetic: 14.4 us -> 33 us
  between operations: 15.6 us -> 2.16 us
    pallas_call x0 -> x2, Pallas kernels: none -> 517 us  [the longest x1 260 us: gather_all(): pl.pallas_call(functools.partial(gather_kernel, layers, chunks), out_shap...]
    all_gather x8 -> x0, waiting for transfers between devices: 387 us -> none  [the longest x2 121 us: gather_weights(): lax.all_gather(expand, ('dp', 'fsdp'), axis=0, tiled=True)]
    unnamed x11 -> x0, waiting for transfers between devices: 379 us -> none
    reduce_scatter x1 -> x0, waiting for transfers between devices: 259 us -> none  [sum_grads(): lax.psum_scatter(jnp.concatenate([rows_product(attn_in, proj_grad), rows_...]
    concatenate x2, local copies, waits for them, and re-layouts: 61.5 us -> 3.59 us  [the longest x1 2.96 us: per_device_linked(): jnp.concatenate([inproj_two[:, 2 * width:], gains, jnp.zeros((rows, PIECE...]
    unnamed x1 -> x0, blocking collectives: 42.3 us -> none
    dot_general x8 -> x0, matrix products: 32.6 us -> none  [rows_product(): lax.dot_general(left, right, (((0,), (0,)), ((), ())), preferred_element_...]
    unnamed x222 -> x204, local copies, waits for them, and re-layouts: 17.6 us -> 27.6 us
  transfers between devices with their start and end apart: 10 -> 0, of which waited for: 10 -> 0; matrix products, arithmetic and copies ran while one was open for 9% -> 0% of each run, Pallas kernels for 0% -> 0%
where the time goes in v1:
time: 721 us; the launch traced here: 710 us
  Pallas kernels  517 us (72%)
  local copies, waits for them, and re-layouts  81.1 us (11%)
  matrix products  77 us (11%)
  other arithmetic  33 us (5%)
    pallas_call x1, Pallas kernels, gather_all(): pl.pallas_call(functools.partial(gather_kernel, layers, chunks), out_shap...  260 us
    pallas_call x1, Pallas kernels, scatter_all(): pl.pallas_call(functools.partial(scatter_kernel, layers, chunks), out_sha...  258 us
    dot_general x8, matrix products, cols_product(): lax.dot_general(left, right, (((1,), (1,)), ((), ())), preferred_element_...  30.3 us
    unnamed x204, local copies, waits for them, and re-layouts  27.6 us

profile of v1, /device:TPU:0, one launch (start us, length us, event | category | flops | bytes accessed | tf_op | source)
XLA Modules:
  0.0 710.3 jit_solution(18244283391861938482)
XLA Ops:
  9.7 3.0 concatenate.31.own
  12.7 259.5 %shard_map.254 = bf16[4,2,2,48,18432]{4,3,2,1,0:T(8,128)(2,1)} custom-call(bf16[24,18432]{1,0:T(8,128)(2,1)} %concatenate.31.own), custom_call_target="tpu_custom_call" | custom-call | tf_op jit(solution)/shard_map/pallas_call | solution.py:787
  272.3 2.0 slice.184
  278.3 3.2 convolution_convert_fusion
  285.0 3.3 slice.183
  292.3 1.9 copy.100
  294.2 2.0 fusion.114
  297.6 3.8 fusion.14
  301.5 5.6 fusion.115
  310.7 1.9 copy.79
  312.6 1.8 pad_maximum_fusion.3
  314.4 1.9 copy.77
  316.4 1.9 copy.78
  318.3 2.2 fusion.41
  323.8 1.9 copy.103
  325.8 2.2 fusion.116
  328.3 3.8 fusion.6
  332.1 6.4 fusion.48
  338.5 5.3 fusion.32
  343.9 4.5 multiply_reduce_fusion.2
  351.5 2.5 convolution_convert_fusion.3
  354.0 1.9 copy.83
  356.0 2.8 fusion.89
  360.2 1.7 copy.117
  361.9 1.9 copy.119
  363.9 1.7 copy.88
  365.6 3.5 multiply_reduce_fusion.1
  372.5 2.5 multiply_reduce_fusion.3
  375.1 1.9 copy.101
  377.0 1.9 copy.102
  381.1 1.7 fusion.109
  384.3 5.3 fusion.25
  389.7 4.5 multiply_reduce_fusion.4
  401.3 2.5 convolution_convert_fusion.2
  403.8 1.9 copy.89
  405.7 1.8 fusion.92
  409.0 1.7 copy.120
  410.8 1.9 copy.118
  412.7 1.7 copy.97
  414.4 2.4 multiply_reduce_fusion
  422.2 1.8 constant_dynamic-update-slice_fusion.11
  424.0 2.0 constant_dynamic-update-slice_fusion.10
  426.0 1.9 constant_dynamic-update-slice_fusion.9
  430.8 2.1 constant_dynamic-update-slice_fusion.5
  436.6 2.1 constant_dynamic-update-slice_fusion.rights
  439.0 3.2 fusion.80
  444.0 257.6 %shard_map.255 = f32[24,18432]{1,0:T(8,128)} custom-call(bf16[8,256,768]{2,1,0:T(8,128)(2,1)} %bitcast_dynamic-update-slice_fusion.lefts, bf16[256,18432]{1,0:T(8,128)(2,1)} %constant_dynamic-update-slice_fusion.rights, f32[8,768]{1,0:T(8,128)} %concatenate.37.gains), custom_call_target="tpu_custom_call" | custom-call | tf_op jit(solution)/shard_map/pallas_call | solution.py:810
  702.4 2.7 add_add_fusion.4
  (287 shorter events, 68.5 us)
Async XLA Ops:
  1.8 286.5 %copy-start.64 = (f32[256]{0:T(256)}, f32[256]{0:T(256)S(1)}, u32[]{:S(2)}) copy-start(f32[256]{0:T(256)S(1)} %broadcast_multiply_fusion.3) | copy-start | bytes 3076
  3.6 284.7 %copy-start.66 = (f32[256]{0:T(256)}, f32[256]{0:T(256)S(1)}, u32[]{:S(2)}) copy-start(f32[256]{0:T(256)S(1)} %fusion.85) | copy-start | bytes 3076
  272.2 6.0 copy-start.7
  278.3 10.1 %copy-start.55 = (f32[768]{0:T(1024)}, f32[768]{0:T(1024)S(1)}, u32[]{:S(2)}) copy-start(f32[768]{0:T(1024)S(1)} %convert_reduce_fusion.4) | copy-start | bytes 9220
  285.0 4.3 copy-start.13
  285.0 4.3 copy-start.19
  285.0 4.3 copy-start.21
  296.2 5.2 copy-start.9
  301.4 5.7 copy-start.25
  301.4 6.6 copy-start.31
  301.4 6.5 copy-start.49
  301.4 6.5 copy-start.59
  318.3 3.9 copy-start.44
  328.0 21.0 %copy-start.5 = (f32[256,768]{1,0:T(8,128)}, f32[256,768]{1,0:T(8,128)S(1)}, u32[]{:S(2)}) copy-start(f32[256,768]{1,0:T(8,128)S(1)} %get-tuple-element.60) | copy-start | bytes 2359300
  328.0 20.9 %copy-start.73 = (f32[256]{0:T(256)}, f32[256]{0:T(256)S(1)}, u32[]{:S(2)}) copy-start(f32[256]{0:T(256)S(1)} %broadcast_multiply_fusion) | copy-start | bytes 3076
  328.3 20.7 %copy-start.84 = (f32[256]{0:T(256)}, f32[256]{0:T(256)S(1)}, u32[]{:S(2)}) copy-start(f32[256]{0:T(256)S(1)} %fusion.88) | copy-start | bytes 3076
  332.1 6.4 copy-start.28
  332.1 6.4 copy-start.17
  343.9 4.5 copy-start.35
  365.6 3.6 copy-start.15
  365.6 3.6 copy-start.54
  378.9 5.4 copy-start.26
  384.3 5.3 copy-start.10
  384.3 5.3 copy-start.63
  384.3 5.3 copy-start.69
  384.3 5.3 copy-start.80
  389.7 4.5 copy-start.37
  389.7 5.1 copy-start.89
  395.1 3.7 copy-start.48
  395.2 4.4 copy-start.6
  395.2 4.4 copy-start.58
  395.2 4.4 copy-start.74
  395.2 4.4 copy-start.85
  396.1 5.2 copy-start.11
  396.1 4.4 copy-start.18
  418.5 9.4 %copy-start.34 = (bf16[256,384]{1,0:T(8,128)(2,1)S(1)}, bf16[256,384]{1,0:T(8,128)(2,1)}, u32[]{:S(2)}) copy-start(bf16[256,384]{1,0:T(8,128)(2,1)} %copy.120) | copy-start | bytes 589828
  418.9 9.7 %copy-start.39 = (bf16[256,768]{1,0:T(8,128)(2,1)S(1)}, bf16[256,768]{1,0:T(8,128)(2,1)}, u32[]{:S(2)}) copy-start(bf16[256,768]{1,0:T(8,128)(2,1)} %copy.100) | copy-start | bytes 1179652
  418.9 10.6 %copy-start.38 = (bf16[256,3072]{1,0:T(8,128)(2,1)S(1)}, bf16[256,3072]{1,0:T(8,128)(2,1)}, u32[]{:S(2)}) copy-start(bf16[256,3072]{1,0:T(8,128)(2,1)} %copy-done.37) | copy-start | bytes 4718596
  424.0 6.8 copy-start.27
  430.8 3.8 copy-start.41
  430.8 4.6 copy-start.36
  432.9 3.7 copy-start.29
  439.0 4.3 copy-start.75
  439.0 4.3 copy-start.76
  439.0 4.3 copy-start.77
  701.6 5.2 slice-start
  701.6 5.2 slice-start.1
  701.6 5.9 copy-start.8
  (46 other events, 85.0 us)

commit v2 on v0

--- a/solution.py
+++ b/solution.py
@@ -1,8 +1,12 @@
+import functools
 import math
+import types
 
 import jax
 import jax.numpy as jnp
 from jax import lax
+from jax.experimental import pallas as pl
+from jax.experimental.pallas import tpu as pltpu
 from jax.sharding import PartitionSpec as P
 
 HEADS = 12
@@ -273,9 +277,1160 @@
     )
 
 
+PIECE = 384
+CHUNK = 2 * PIECE
+CHUNKS = 24
+REGIONS = 28
+MESH = pl.DeviceIdType.MESH
+FULL = slice(None)
+GATHER_LAGS = (0, 2, 4, 6, 9, 12, 13)
+SCATTER_LAGS = (0, 3, 5, 6, 7, 8, 10)
+FIRST_TURN = 33
+TICKS = FIRST_TURN + CHUNKS + SCATTER_LAGS[-1]
+
+
+def when(condition, body):
+    if isinstance(condition, bool):
+        if condition:
+            body()
+    else:
+        pl.when(condition)(body)
+
+
+class Seat:
+    def __init__(self, layers):
+        self.layers = layers
+        self.z = lax.axis_index("dp")
+        place = lax.axis_index("fsdp")
+        self.core = lax.rem(place, 2)
+        self.x = lax.rem(lax.div(place, 2), 2)
+        self.y = lax.div(place, 4)
+        self.partner = (self.z, place + 1 - 2 * self.core)
+        self.across_x = (self.z, place + 2 - 4 * self.x)
+        self.across_y = (self.z, place + 4 - 8 * self.y)
+        self.up = (self.z + 1, place)
+        self.down = (self.z - 1, place)
+        self.has_up = self.z < layers - 1
+        self.has_down = self.z > 0
+
+    def signal(self, semaphore, device):
+        pl.semaphore_signal(semaphore, inc=1, device_id=device, device_id_type=MESH)
+
+    def greet(self):
+        barrier = pltpu.get_barrier_semaphore()
+        for other in (self.partner, self.across_x, self.across_y):
+            self.signal(barrier, other)
+        when(self.has_up, lambda: self.signal(barrier, self.up))
+        when(self.has_down, lambda: self.signal(barrier, self.down))
+        inner = self.has_up & self.has_down
+        when(inner, lambda: pl.semaphore_wait(barrier, 5))
+        when(jnp.logical_not(inner), lambda: pl.semaphore_wait(barrier, 4))
+
+    def give(self, credit, which):
+        self.signal(credit.at[which, 0], self.across_x)
+        self.signal(credit.at[which, 1], self.across_y)
+        when(self.has_up, lambda: self.signal(credit.at[which, 2], self.up))
+        when(self.has_down, lambda: self.signal(credit.at[which, 3], self.down))
+
+    def take(self, credit, which):
+        pl.semaphore_wait(credit.at[which, 0], 1)
+        pl.semaphore_wait(credit.at[which, 1], 1)
+        when(self.has_down, lambda: pl.semaphore_wait(credit.at[which, 2], 1))
+        when(self.has_up, lambda: pl.semaphore_wait(credit.at[which, 3], 1))
+
+
+def columns_of(start, size):
+    return pl.ds(pl.multiple_of(start, 128), size)
+
+
+def remote(source, target, send_sem, recv_sem, device):
+    return pltpu.make_async_remote_copy(
+        src_ref=source,
+        dst_ref=target,
+        send_sem=send_sem,
+        recv_sem=recv_sem,
+        device_id=device,
+        device_id_type=MESH,
+    )
+
+
+def colour_of(chunk):
+    step = lax.rem(chunk, 8)
+    return jnp.where(
+        (step == 2) | (step == 7), 2, jnp.where((step == 1) | (step == 4) | (step == 6), 1, 0)
+    )
+
+
+class Gather:
+    def __init__(self, seat, m):
+        self.seat, self.m = seat, m
+        self.pre_sem, self.recv_sem, self.send_sem = m.pre_sem, m.gather_recv, m.gather_send
+
+    def window(self, chunk, zs, ys, xs, core=None):
+        core = self.seat.core if core is None else core
+        return self.m.held.at[zs, ys, xs, :, columns_of(chunk * CHUNK + core * PIECE, PIECE)]
+
+    def shard(self, ref, chunk, core):
+        rows = pl.ds(pl.multiple_of(32 * lax.div(chunk, 4), 32), self.m.total.shape[0])
+        return ref.at[rows, columns_of(CHUNK * lax.rem(chunk, 4) + PIECE * core, PIECE)]
+
+    def swap(self, chunk, core):
+        return remote(
+            self.shard(self.m.own_rows, chunk, core),
+            self.shard(self.m.other_rows, chunk, core),
+            self.pre_sem.at[0, chunk],
+            self.pre_sem.at[1, chunk],
+            self.seat.partner,
+        )
+
+    def copy(self, chunk, zs, ys, xs, kind, arrival, device):
+        window = self.window(chunk, zs, ys, xs)
+        return remote(
+            window, window, self.send_sem.at[chunk, kind], self.recv_sem.at[chunk, arrival], device
+        )
+
+    def up(self, chunk, origin, ys, xs):
+        return self.copy(chunk, origin, ys, xs, origin, origin, self.seat.up)
+
+    def down(self, chunk, origin, ys, xs):
+        return self.copy(chunk, origin, ys, xs, 4 + origin, origin, self.seat.down)
+
+    def merge(self, chunk):
+        seat = self.seat
+        self.swap(chunk, 1 - seat.core).wait_send()
+        self.swap(chunk, seat.core).wait_recv()
+        mine = self.shard(self.m.own_rows, chunk, seat.core)[...].astype(jnp.float32)
+        theirs = self.shard(self.m.other_rows, chunk, seat.core)[...].astype(jnp.float32)
+        first = seat.core == 0
+        both = jnp.concatenate(
+            [jnp.where(first, mine, theirs), jnp.where(first, theirs, mine)], axis=0
+        )
+        columns = columns_of(chunk * CHUNK + seat.core * PIECE, PIECE)
+        self.m.held[seat.z, seat.y, seat.x, :, columns] = both.astype(jnp.bfloat16)
+
+    def start_z(self, chunk, ys, xs):
+        seat = self.seat
+        when(seat.has_up, lambda: self.up(chunk, seat.z, ys, xs).start())
+        when(seat.has_down, lambda: self.down(chunk, seat.z, ys, xs).start())
+
+    def relay_z(self, chunk, step, ys, xs):
+        seat = self.seat
+        below, above = seat.z - 1 - step, seat.z + 1 + step
+
+        def from_below():
+            self.up(chunk, below, ys, xs).wait_recv()
+            when(seat.has_up, lambda: self.up(chunk, below, ys, xs).start())
+
+        def from_above():
+            self.down(chunk, above, ys, xs).wait_recv()
+            when(seat.has_down, lambda: self.down(chunk, above, ys, xs).start())
+
+        when(below >= 0, from_below)
+        when(above <= seat.layers - 1, from_above)
+
+    def side(self, chunk, axis, zs, other):
+        seat = self.seat
+        if axis == "x":
+            return self.copy(chunk, zs, other, seat.x, 8, 4, seat.across_x)
+        return self.copy(chunk, zs, seat.y, other, 9, 5, seat.across_y)
+
+    def side_arrives(self, chunk, axis, zs, other):
+        seat = self.seat
+        if axis == "x":
+            self.copy(chunk, zs, other, 1 - seat.x, 8, 4, seat.across_x).wait_recv()
+        else:
+            self.copy(chunk, zs, 1 - seat.y, other, 9, 5, seat.across_y).wait_recv()
+
+    def to_partner(self, chunk):
+        return self.copy(chunk, FULL, FULL, FULL, 10, 6, self.seat.partner)
+
+    def stage(self, chunk, number):
+        seat = self.seat
+        y, x = seat.y, seat.x
+
+        def z_first(first, second, own_first):
+            if number == 0:
+                self.start_z(chunk, y, x)
+            elif number <= 3:
+                self.relay_z(chunk, number - 1, y, x)
+            if number == 3:
+                self.side(chunk, first, FULL, own_first).start()
+            if number == 4:
+                self.side_arrives(chunk, first, FULL, own_first)
+                self.side(chunk, second, FULL, FULL).start()
+            if number == 5:
+                self.side_arrives(chunk, second, FULL, FULL)
+
+        def z_last():
+            if number == 0:
+                self.side(chunk, "x", seat.z, y).start()
+            if number == 1:
+                self.side_arrives(chunk, "x", seat.z, y)
+                self.side(chunk, "y", seat.z, FULL).start()
+            if number == 2:
+                self.side_arrives(chunk, "y", seat.z, FULL)
+                self.start_z(chunk, FULL, FULL)
+            if number >= 3:
+                self.relay_z(chunk, number - 3, FULL, FULL)
+
+        if number == 0:
+            self.merge(chunk)
+        if number <= 5:
+            colour = colour_of(chunk)
+            when(colour == 0, lambda: z_first("x", "y", y))
+            when(colour == 1, lambda: z_first("y", "x", x))
+            when(colour == 2, z_last)
+        if number == 5:
+            self.to_partner(chunk).start()
+        if number == 6:
+            window = self.window(chunk, FULL, FULL, FULL, 1 - seat.core)
+            remote(
+                window, window, self.send_sem.at[chunk, 10], self.recv_sem.at[chunk, 6], seat.partner
+            ).wait_recv()
+
+    def drain(self, chunk):
+        seat = self.seat
+        y, x = seat.y, seat.x
+
+        def z_sends(ys, xs):
+            for origin in range(seat.layers):
+                when(
+                    seat.has_up & (seat.z >= origin),
+                    lambda: self.up(chunk, origin, ys, xs).wait_send(),
+                )
+                when(
+                    seat.has_down & (seat.z <= origin),
+                    lambda: self.down(chunk, origin, ys, xs).wait_send(),
+                )
+
+        def z_first(first, second, own_first):
+            z_sends(y, x)
+            self.side(chunk, first, FULL, own_first).wait_send()
+            self.side(chunk, second, FULL, FULL).wait_send()
+
+        def z_last():
+            z_sends(FULL, FULL)
+            self.side(chunk, "x", seat.z, y).wait_send()
+            self.side(chunk, "y", seat.z, FULL).wait_send()
+
+        colour = colour_of(chunk)
+        when(colour == 0, lambda: z_first("x", "y", y))
+        when(colour == 1, lambda: z_first("y", "x", x))
+        when(colour == 2, z_last)
+        self.to_partner(chunk).wait_send()
+
+    def round(self, i):
+        for number in reversed(range(7)):
+            chunk = i - GATHER_LAGS[number]
+            when((chunk >= 0) & (chunk < CHUNKS), functools.partial(self.stage, chunk, number))
+
+
+def chunk_at(turn):
+    chunk = turn - 23
+    for end, shift in ((23, -19), (20, -15), (19, -10), (15, -2), (11, 4), (9, 7), (8, 12), (4, 20)):
+        chunk = jnp.where(turn < end, turn + shift, chunk)
+    return chunk
+
+
+def region_at(turn):
+    region = turn - 19
+    for end, shift in ((23, -14), (19, -6), (15, 0), (13, 3), (12, 8), (8, 16), (4, 24)):
+        region = jnp.where(turn < end, turn + shift, region)
+    return jnp.where(turn == 13, 13, region)
+
+
+class Scatter:
+    def __init__(self, seat, m, fill):
+        self.seat, self.m, self.fill = seat, m, fill
+        self.recv_sem, self.send_sem = m.scatter_recv, m.scatter_send
+
+    def part(self, turn):
+        return columns_of(region_at(turn) * CHUNK + PIECE, PIECE)
+
+    def landing(self, turn):
+        return columns_of(region_at(turn) * CHUNK, PIECE)
+
+    def rare(self, turn):
+        return 2 * lax.div(turn, 8) + lax.div(lax.rem(turn, 8), 7)
+
+    def sent(self, turn, zs, ys, xs, target, kind, arrival, device):
+        return remote(
+            self.m.held.at[zs, ys, xs, :, self.part(turn)],
+            target,
+            self.send_sem.at[turn, kind],
+            self.recv_sem.at[turn, arrival],
+            device,
+        )
+
+    def add(self, turn, zs, ys, xs, landed):
+        columns = self.part(turn)
+        value = self.m.held[zs, ys, xs, :, columns].astype(jnp.float32)
+        value = value + landed[...].astype(jnp.float32)
+        self.m.held[zs, ys, xs, :, columns] = value.astype(jnp.bfloat16)
+
+    def side(self, turn, axis, zs, other, target):
+        seat = self.seat
+        if axis == "x":
+            return self.sent(turn, zs, other, 1 - seat.x, target, 0, 0, seat.across_x)
+        return self.sent(turn, zs, 1 - seat.y, other, target, 1, 1, seat.across_y)
+
+    def finish_side(self, turn, axis, zs, other, target):
+        seat = self.seat
+        self.side(turn, axis, zs, other, target).wait_recv()
+        if axis == "x":
+            self.add(turn, zs, other, seat.x, target)
+        else:
+            self.add(turn, zs, seat.y, other, target)
+
+    def first_spot(self, turn):
+        return self.m.held.at[:, 0, :, :, self.landing(turn)]
+
+    def second_spot(self, turn):
+        return self.m.held.at[:, 1, 0, :, self.landing(turn)]
+
+    def late_z_spot(self, turn, goal):
+        return self.m.held.at[goal, 1, 1, :, self.landing(turn)]
+
+    def late_own_spot(self, turn):
+        return self.m.extra.at[turn]
+
+    def early_z_spot(self, turn, goal):
+        return self.m.held.at[goal, :, :, :, self.landing(turn)]
+
+    def early_own_spot(self, turn):
+        return self.m.extra_four.at[self.rare(turn)]
+
+    def early_y_spot(self, turn):
+        return self.m.extra_two.at[self.rare(turn)]
+
+    def early_x_spot(self, turn):
+        return self.m.extra.at[turn]
+
+    def step_z(self, turn, step, spot, own_spot, ys, xs):
+        seat = self.seat
+        layers = seat.layers
+
+        def send_up(goal):
+            return self.sent(turn, goal, ys, xs, spot(turn, goal), 2 + goal, 2 + goal, seat.up)
+
+        def send_down(goal):
+            return self.sent(turn, goal, ys, xs, spot(turn, goal), 2 + goal, 2 + goal, seat.down)
+
+        def send_down_own(goal):
+            return self.sent(
+                turn, goal, ys, xs, own_spot(turn), 2 + goal, 2 + layers, seat.down
+            )
+
+        def arrived(goal, window, arrival):
+            remote(
+                window,
+                window,
+                self.send_sem.at[turn, 0],
+                self.recv_sem.at[turn, 2 + arrival],
+                seat.partner,
+            ).wait_recv()
+            self.add(turn, goal, ys, xs, window)
+
+        def upward():
+            for goal in range(1, layers):
+
+                def one(goal=goal):
+                    when(seat.has_down, lambda: arrived(goal, spot(turn, goal), goal))
+                    when(seat.z < goal, lambda: send_up(goal).start())
+
+                when(seat.z <= goal, one)
+
+        def downward():
+            for goal in range(layers - 1):
+
+                def one(goal=goal):
+                    when(
+                        seat.has_up & (seat.z != goal),
+                        lambda: arrived(goal, spot(turn, goal), goal),
+                    )
+                    when(
+                        seat.has_up & (seat.z == goal),
+                        lambda: arrived(goal, own_spot(turn), layers),
+                    )
+                    when(seat.z > goal + 1, lambda: send_down(goal).start())
+                    when(seat.z == goal + 1, lambda: send_down_own(goal).start())
+
+                when(seat.z >= goal, one)
+
+        when(seat.z == step, upward)
+        when(seat.z == layers - 1 - step, downward)
+
+    def finished(self, turn):
+        return self.m.finished.at[lax.rem(turn, 4)]
+
+    def hand_over(self, turn):
+        rows = self.m.total.shape[0]
+        theirs = pl.ds(pl.multiple_of((1 - self.seat.core) * rows, 8), rows)
+        columns = columns_of(chunk_at(turn) * CHUNK + self.seat.core * PIECE, PIECE)
+        return remote(
+            self.finished(turn).at[theirs],
+            self.m.total.at[:, columns],
+            self.send_sem.at[turn, 6],
+            self.recv_sem.at[turn, 7],
+            self.seat.partner,
+        )
+
+    def stage(self, turn, number):
+        seat = self.seat
+        y, x, z = seat.y, seat.x, seat.z
+
+        def z_last(first, second, own_second):
+            if number == 0:
+                self.side(turn, first, FULL, FULL, self.first_spot(turn)).start()
+            if number == 1:
+                self.finish_side(turn, first, FULL, FULL, self.first_spot(turn))
+                self.side(turn, second, FULL, own_second, self.second_spot(turn)).start()
+            if number == 2:
+                self.finish_side(turn, second, FULL, own_second, self.second_spot(turn))
+            if number >= 2:
+                self.step_z(turn, number - 2, self.late_z_spot, self.late_own_spot, y, x)
+
+        def z_first():
+            if number <= 3:
+                self.step_z(turn, number, self.early_z_spot, self.early_own_spot, FULL, FULL)
+            if number == 3:
+                self.side(turn, "y", z, FULL, self.early_y_spot(turn)).start()
+            if number == 4:
+                self.finish_side(turn, "y", z, FULL, self.early_y_spot(turn))
+                self.side(turn, "x", z, y, self.early_x_spot(turn)).start()
+            if number == 5:
+                self.finish_side(turn, "x", z, y, self.early_x_spot(turn))
+
+        if number == 0:
+            self.fill(turn, chunk_at(turn), self.part(turn))
+        if number <= 5:
+            colour = colour_of(turn)
+            when(colour == 0, lambda: z_last("y", "x", y))
+            when(colour == 1, lambda: z_last("x", "y", x))
+            when(colour == 2, z_first)
+        if number == 5:
+            rows = self.m.total.shape[0]
+            ready = self.finished(turn)
+            ready[...] = self.m.held[z, y, x, :, self.part(turn)].astype(jnp.float32)
+            mine = pl.ds(pl.multiple_of(seat.core * rows, 8), rows)
+            columns = columns_of(chunk_at(turn) * CHUNK + seat.core * PIECE, PIECE)
+            self.m.total[:, columns] = ready[mine, :]
+            self.hand_over(turn).start()
+        if number == 6:
+            self.hand_over(turn).wait_send()
+            columns = columns_of(chunk_at(turn) * CHUNK + (1 - seat.core) * PIECE, PIECE)
+            window = self.m.total.at[:, columns]
+            remote(
+                window, window, self.send_sem.at[turn, 6], self.recv_sem.at[turn, 7], seat.partner
+            ).wait_recv()
+            self.drain(turn)
+
+    def drain(self, turn):
+        seat = self.seat
+        y, x, z = seat.y, seat.x, seat.z
+
+        def z_sends(spot, ys, xs):
+            for goal in range(seat.layers):
+
+                def one(goal=goal):
+                    self.sent(
+                        turn, goal, ys, xs, spot(turn, goal), 2 + goal, 2 + goal, seat.partner
+                    ).wait_send()
+
+                when(seat.z != goal, one)
+
+        def z_last(first, second, own_second):
+            self.side(turn, first, FULL, FULL, self.first_spot(turn)).wait_send()
+            self.side(turn, second, FULL, own_second, self.second_spot(turn)).wait_send()
+            z_sends(self.late_z_spot, y, x)
+
+        def z_first():
+            z_sends(self.early_z_spot, FULL, FULL)
+            self.side(turn, "y", z, FULL, self.early_y_spot(turn)).wait_send()
+            self.side(turn, "x", z, y, self.early_x_spot(turn)).wait_send()
+
+        colour = colour_of(turn)
+        when(colour == 0, lambda: z_last("y", "x", y))
+        when(colour == 1, lambda: z_last("x", "y", x))
+        when(colour == 2, z_first)
+
+    def round(self, i):
+        for number in reversed(range(7)):
+            turn = i - SCATTER_LAGS[number]
+            when((turn >= 0) & (turn < CHUNKS), functools.partial(self.stage, turn, number))
+
+
+def nn_product(left, right):
+    return lax.dot_general(
+        left, right, (((1,), (0,)), ((), ())), preferred_element_type=jnp.float32
+    )
+
+
+def nt_product(left, right):
+    return lax.dot_general(
+        left, right, (((1,), (1,)), ((), ())), preferred_element_type=jnp.float32
+    )
+
+
+def tn_product(left, right):
+    return lax.dot_general(
+        left, right, (((0,), (0,)), ((), ())), preferred_element_type=jnp.float32
+    )
+
+
+def normal(value):
+    centred = value - jnp.mean(value, axis=-1, keepdims=True)
+    spread = jnp.mean(centred * centred, axis=-1, keepdims=True)
+    rate = lax.rsqrt(spread + 1e-05)
+    return centred * rate, rate
+
+
+def loop(count, body):
+    lax.fori_loop(0, count, lambda i, c: (body(i), c)[1], 0)
+
+
+class Layers:
+    def __init__(self, seat, m):
+        self.seat, self.m = seat, m
+        self.width = m.block.shape[1]
+        self.scale = 1.0 / math.sqrt(self.width // HEADS)
+
+    def weight(self, chunk):
+        return self.m.held[:, :, :, :, columns_of(chunk * CHUNK, CHUNK)].reshape(
+            self.width, CHUNK
+        )
+
+    def gain(self, row):
+        return self.m.gains[pl.ds(row, 1), :]
+
+    def begin(self):
+        m = self.m
+        columns = m.held[:, :, :, :, pl.ds(PIECE, 128)].reshape(self.width, 128)
+        turned = jnp.transpose(columns.astype(jnp.float32))
+        m.gains[...] = turned[:8]
+        m.gain_grads[...] = jnp.zeros_like(m.gain_grads)
+        segment = m.segment[...].astype(jnp.float32)
+        tokens = segment.shape[1]
+        across = jnp.broadcast_to(segment, (tokens, tokens))
+        along = jnp.transpose(across)
+        later = lax.broadcasted_iota(jnp.int32, (tokens, tokens), 1)
+        now = lax.broadcasted_iota(jnp.int32, (tokens, tokens), 0)
+        allowed = (along == across) & (later <= now)
+        m.allowed[...] = jnp.where(allowed, 1.0, 0.0)
+        m.block_load.wait()
+        value = m.mixed_grad[...].astype(jnp.float32)
+        m.entered[0] = value
+        m.attn_in[0] = (normal(value)[0] * self.gain(0)).astype(jnp.bfloat16)
+
+    def project(self, layer, part, chunk):
+        m = self.m
+        value = nn_product(m.attn_in[layer], self.weight(chunk))
+        m.proj[layer, :, columns_of(part * CHUNK, CHUNK)] = value.astype(jnp.bfloat16)
+
+    def project_fresh(self):
+        m = self.m
+        half = self.width // 2
+        weight = m.held[:, :, :, :, pl.ds(0, PIECE)].reshape(self.width, PIECE)
+        value = nn_product(m.attn_in[1], weight)
+        m.proj[1, :, pl.ds(2 * self.width + half, half)] = value.astype(jnp.bfloat16)
+        m.proj[1, :, pl.ds(2 * self.width, half)] = m.proj[0, :, pl.ds(2 * self.width, half)]
+
+    def heads(self, layer, pair):
+        m = self.m
+        parts = []
+        for i in range(3):
+            parts.append(m.proj[layer, :, columns_of(i * self.width + pair * 128, 128)])
+        return parts
+
+    def own_lanes(self, which):
+        lane = lax.broadcasted_iota(jnp.int32, (self.m.block.shape[0], 128), 1)
+        return (lane < 64) if which == 0 else (lane >= 64)
+
+    def only(self, which, value):
+        return jnp.where(self.own_lanes(which), value, jnp.zeros_like(value))
+
+    def probabilities(self, query, keys):
+        scores = nt_product(query, keys) * self.scale
+        scores = jnp.where(self.m.allowed[...] > 0.5, scores, -1000000000.0)
+        highest = jnp.max(scores, axis=-1, keepdims=True)
+        powers = jnp.exp(scores - highest)
+        return powers * (1.0 / jnp.sum(powers, axis=-1, keepdims=True))
+
+    def attend(self, layer):
+        m = self.m
+
+        def pair(p):
+            query, keys, values = self.heads(layer, p)
+            mixed = []
+            for which in range(2):
+                probs = self.probabilities(self.only(which, query), keys)
+                mixed.append(nn_product(probs.astype(jnp.bfloat16), values))
+            m.mixed[layer, :, columns_of(p * 128, 128)] = jnp.where(
+                self.own_lanes(0), mixed[0], mixed[1]
+            ).astype(jnp.bfloat16)
+
+        loop(HEADS // 2, pair)
+
+    def project_out(self, layer, chunk):
+        m = self.m
+        middle = m.entered[layer] + nt_product(m.mixed[layer], self.weight(chunk))
+        m.middle[layer] = middle
+        m.mlp_in[layer] = (normal(middle)[0] * self.gain(2 * layer + 1)).astype(jnp.bfloat16)
+
+    def expand(self, layer, part, chunk):
+        m = self.m
+        value = nn_product(m.mlp_in[layer], self.weight(chunk))
+        root = math.sqrt(2.0 / math.pi)
+        square = value * value
+        bend = jnp.tanh(root * value * (1.0 + 0.044715 * square))
+        columns = columns_of(part * CHUNK, CHUNK)
+        m.active[layer, :, columns] = (0.5 * value * (1.0 + bend)).astype(jnp.bfloat16)
+        slope = 0.5 * (1.0 + bend) + 0.5 * value * (1.0 - bend * bend) * (
+            root * (1.0 + 3.0 * 0.044715 * square)
+        )
+        m.slope[layer, :, columns] = slope.astype(jnp.bfloat16)
+
+    def shrink(self, layer, part, chunk):
+        m = self.m
+        term = nt_product(m.active[layer, :, columns_of(part * CHUNK, CHUNK)], self.weight(chunk))
+
+        @pl.when(part == 0)
+        def _():
+            m.output[...] = m.middle[layer] + term
+
+        @pl.when(part > 0)
+        def _():
+            m.output[...] += term
+
+        @pl.when((part == 3) & (layer == 0))
+        def _():
+            value = m.output[...]
+            m.entered[1] = value
+            m.attn_in[1] = (normal(value)[0] * self.gain(2)).astype(jnp.bfloat16)
+
+    def forward(self, chunk):
+        second = chunk >= 13
+        layer = jnp.where(second, 1, 0)
+        begins = [jnp.where(second, b, a) for a, b in ((1, 13), (4, 15), (5, 16), (9, 20))]
+        when(chunk == 0, self.begin)
+        when(
+            (chunk >= begins[0]) & (chunk < begins[1]),
+            lambda: self.project(layer, chunk - begins[0], chunk),
+        )
+        when(chunk == 14, self.project_fresh)
+        when(chunk == begins[1] - 1, lambda: self.attend(layer))
+        when(chunk == begins[1], lambda: self.project_out(layer, chunk))
+        when(
+            (chunk >= begins[2]) & (chunk < begins[3]),
+            lambda: self.expand(layer, chunk - begins[2], chunk),
+        )
+        when(
+            (chunk >= begins[3]) & (chunk < begins[3] + 4),
+            lambda: self.shrink(layer, chunk - begins[3], chunk),
+        )
+
+
+    def exchange(self, layer, item):
+        m = self.m
+        width = self.width
+        pairs = (
+            (m.out_low.at[layer], m.other_out_low),
+            (m.active.at[layer], m.other_active),
+            (m.mlp_in.at[layer], m.other_mlp_in),
+            (m.slope.at[layer], m.other_slope),
+            (m.mixed.at[layer], m.other_mixed),
+            (m.branch.at[layer], m.other_branch),
+            (m.attn_in.at[layer], m.other_attn_in.at[layer]),
+            (m.proj.at[layer, :, pl.ds(0, 2 * width)], m.other_proj.at[:, pl.ds(0, 2 * width)]),
+            (m.proj.at[0, :, pl.ds(2 * width, width)], m.other_proj.at[:, pl.ds(2 * width, width)]),
+            (m.proj.at[1, :, pl.ds(2 * width + width // 2, width // 2)], m.other_fresh),
+            (m.gain_grads, m.other_gain_grads),
+        )
+        source, target = pairs[item]
+        return remote(
+            source,
+            target,
+            m.pair_sem.at[0, layer, item],
+            m.pair_sem.at[1, layer, item],
+            self.seat.partner,
+        )
+
+    def hidden_back(self, layer):
+        m = self.m
+
+        def part(j):
+            columns = columns_of(j * CHUNK, CHUNK)
+            grad = nn_product(
+                m.out_low[layer], self.weight(jnp.where(layer == 1, 20, 9) + j)
+            )
+            slope = m.slope[layer, :, columns].astype(jnp.float32)
+            m.slope[layer, :, columns] = (grad * slope).astype(jnp.bfloat16)
+
+        loop(4, part)
+
+    def norm_back(self, value, grad, row):
+        m = self.m
+        unit, rate = normal(value)
+        m.gain_grads[pl.ds(row, 1), :] = jnp.sum(grad * unit, axis=0, keepdims=True)
+        scaled = grad * self.gain(row)
+        return rate * (
+            scaled
+            - jnp.mean(scaled, axis=-1, keepdims=True)
+            - unit * jnp.mean(scaled * unit, axis=-1, keepdims=True)
+        )
+
+    def middle_back(self, layer):
+        m = self.m
+        first = jnp.where(layer == 1, 16, 5)
+        grad = None
+        for j in range(4):
+            term = nt_product(m.slope[layer, :, pl.ds(j * CHUNK, CHUNK)], self.weight(first + j))
+            grad = term if grad is None else grad + term
+        m.grad[...] += self.norm_back(m.middle[layer], grad, 2 * layer + 1)
+        low = m.grad[...].astype(jnp.bfloat16)
+        m.branch[layer] = low
+        chunk = jnp.where(layer == 1, 15, 4)
+        m.mixed_grad[...] = nn_product(low, self.weight(chunk)).astype(jnp.bfloat16)
+
+    def attend_back(self, layer):
+        m = self.m
+        width = self.width
+
+        def pair(p):
+            query, keys, values = self.heads(layer, p)
+            above = m.mixed_grad[:, columns_of(p * 128, 128)]
+            grads = []
+            for which in range(2):
+                probs32 = self.probabilities(self.only(which, query), keys)
+                probs = probs32.astype(jnp.bfloat16)
+                prob_grad = nt_product(self.only(which, above), values)
+                value_grad = tn_product(probs, above)
+                score_grad = probs32 * (
+                    prob_grad - jnp.sum(probs32 * prob_grad, axis=-1, keepdims=True)
+                )
+                low = score_grad.astype(jnp.bfloat16)
+                grads.append(
+                    (
+                        nn_product(low, keys) * self.scale,
+                        tn_product(low, query) * self.scale,
+                        value_grad,
+                    )
+                )
+            query_grad, keys_grad, value_grad = [
+                jnp.where(self.own_lanes(0), one, two) for one, two in zip(*grads)
+            ]
+            m.proj[layer, :, columns_of(p * 128, 128)] = query_grad.astype(jnp.bfloat16)
+            m.proj[layer, :, columns_of(width + p * 128, 128)] = keys_grad.astype(jnp.bfloat16)
+            columns = columns_of(2 * width + p * 128, 128)
+            early = p < HEADS // 4
+            carried = columns_of(lax.rem(p, HEADS // 4) * 128, 128)
+
+            @pl.when(early & (layer == 1))
+            def _():
+                m.carried[:, carried] = value_grad
+
+            @pl.when(early & (layer == 0))
+            def _():
+                m.proj[layer, :, columns] = (value_grad + m.carried[:, carried]).astype(
+                    jnp.bfloat16
+                )
+
+            @pl.when(jnp.logical_not(early))
+            def _():
+                m.proj[layer, :, columns] = value_grad.astype(jnp.bfloat16)
+
+        loop(HEADS // 2, pair)
+
+    def enter_back(self, layer):
+        m = self.m
+        width, half = self.width, self.width // 2
+        first = jnp.where(layer == 1, 13, 1)
+        grad = nt_product(m.proj[layer, :, pl.ds(0, width)], self.weight(first))
+        grad += nt_product(m.proj[layer, :, pl.ds(width, width)], self.weight(first + 1))
+        m.scratch[...] = grad
+
+        @pl.when(layer == 1)
+        def _():
+            weight = m.held[:, :, :, :, pl.ds(0, PIECE)].reshape(width, PIECE)
+            m.scratch[...] += nt_product(m.proj[1, :, pl.ds(2 * width + half, half)], weight)
+
+        @pl.when(layer == 0)
+        def _():
+            m.scratch[...] += nt_product(m.proj[0, :, pl.ds(2 * width, width)], self.weight(3))
+
+        m.grad[...] += self.norm_back(m.entered[layer], m.scratch[...], 2 * layer)
+
+        @pl.when(layer == 1)
+        def _():
+            m.out_low[0] = m.grad[...].astype(jnp.bfloat16)
+
+    def fill(self, turn, chunk, target):
+        m = self.m
+        seat = self.seat
+        second = chunk >= 13
+        layer = jnp.where(second, 1, 0)
+        begins = [jnp.where(second, b, a) for a, b in ((1, 13), (4, 15), (5, 16), (9, 20))]
+        shape = m.held.shape[:4]
+
+        def store(value):
+            m.held[:, :, :, :, target] = value.astype(jnp.bfloat16).reshape(shape + (PIECE,))
+
+        def product(begin, left, other_left, right, other_right):
+            def run():
+                columns = columns_of((chunk - begin) * CHUNK + seat.core * PIECE, PIECE)
+                store(
+                    tn_product(left[...], right[:, columns])
+                    + tn_product(other_left[...], other_right[:, columns])
+                )
+
+            return run
+
+        def arrive(items):
+            for item in items:
+                copy = self.exchange(layer, item)
+                copy.wait_send()
+                copy.wait_recv()
+
+        def arrive_fixed(where, item):
+            copy = self.exchange(where, item)
+            copy.wait_send()
+            copy.wait_recv()
+
+        at_proj = (chunk >= begins[0]) & (chunk < begins[1])
+        at_out = chunk == begins[1]
+        at_expand = (chunk >= begins[2]) & (chunk < begins[3])
+        at_shrink = chunk >= begins[3]
+        at_shrink = at_shrink & (chunk < begins[3] + 4)
+        when(at_shrink & (chunk == begins[3]), lambda: arrive((0, 1)))
+        when(at_expand & (chunk == begins[2]), lambda: arrive((2, 3)))
+        when(at_out, lambda: arrive((4, 5)))
+
+        @pl.when(at_proj & (chunk == begins[0]))
+        def _():
+            arrive((6, 7))
+            when(layer == 1, lambda: arrive_fixed(1, 9))
+            when(layer == 0, lambda: arrive_fixed(0, 8))
+
+        when(
+            at_shrink,
+            product(
+                begins[3], m.out_low.at[layer], m.other_out_low, m.active.at[layer], m.other_active
+            ),
+        )
+        when(
+            at_expand,
+            product(
+                begins[2], m.mlp_in.at[layer], m.other_mlp_in, m.slope.at[layer], m.other_slope
+            ),
+        )
+        when(
+            at_out,
+            product(
+                begins[1], m.branch.at[layer], m.other_branch, m.mixed.at[layer], m.other_mixed
+            ),
+        )
+        when(
+            at_proj,
+            product(
+                begins[0],
+                m.attn_in.at[layer],
+                m.other_attn_in.at[layer],
+                m.proj.at[layer],
+                m.other_proj,
+            ),
+        )
+
+        @pl.when((chunk == 0) & (seat.core == 0))
+        def _():
+            own = m.proj[1, :, pl.ds(2 * self.width + PIECE, PIECE)]
+            store(
+                tn_product(m.attn_in[1], own) + tn_product(m.other_attn_in[1], m.other_fresh[...])
+            )
+
+        @pl.when(chunk == 0)
+        def _():
+            arrive_fixed(0, 10)
+
+        @pl.when((chunk == 0) & (seat.core == 1))
+        def _():
+            both = m.gain_grads[...] + m.other_gain_grads[...]
+            padded = jnp.concatenate(
+                [both, jnp.zeros((120, both.shape[1]), jnp.float32)], axis=0
+            )
+            turned = jnp.transpose(padded)
+            wide = jnp.concatenate(
+                [turned, jnp.zeros((turned.shape[0], PIECE - 128), jnp.float32)], axis=1
+            )
+            store(wide)
+
+    def backward(self, tick):
+        m = self.m
+        seat = self.seat
+
+        def send(layer, *items):
+            for item in items:
+                self.exchange(layer, item).start()
+
+        @pl.when(tick == 20)
+        def _():
+            m.above_load.wait()
+            m.grad[...] = m.out_low[1].astype(jnp.float32)
+
+        when(tick == FIRST_TURN - 1, lambda: send(1, 0, 1, 2, 4, 6))
+
+        @pl.when(tick == 44)
+        def _():
+            pl.semaphore_wait(m.pair_credit.at[0], 1)
+            send(0, 0, 1, 2, 4, 6)
+
+        @pl.when((tick == 36) | (tick == 44))
+        def _():
+            layer = jnp.where(tick == 36, 1, 0)
+            self.hidden_back(layer)
+            send(layer, 3)
+            when(tick == 36, lambda: seat.give(m.credit, 0))
+            when(tick == 44, lambda: seat.give(m.credit, 3))
+
+        @pl.when((tick == 37) | (tick == 46))
+        def _():
+            layer = jnp.where(tick == 37, 1, 0)
+            self.middle_back(layer)
+            send(layer, 5)
+            when(tick == 37, lambda: seat.give(m.credit, 1))
+            when(tick == 46, lambda: seat.give(m.credit, 4))
+
+        @pl.when((tick == 38) | (tick == 48))
+        def _():
+            layer = jnp.where(tick == 38, 1, 0)
+            self.attend_back(layer)
+            send(layer, 7)
+            when(tick == 38, lambda: send(1, 9))
+            when(tick == 48, lambda: send(0, 8))
+
+        @pl.when((tick == 39) | (tick == 50))
+        def _():
+            layer = jnp.where(tick == 39, 1, 0)
+            self.enter_back(layer)
+            when(tick == 39, lambda: seat.give(m.credit, 2))
+            when(tick == 50, lambda: send(0, 10))
+
+
+def whole_kernel(layers, names, *refs):
+    m = types.SimpleNamespace(**dict(zip(names, refs)))
+    seat = Seat(layers)
+    seat.greet()
+    m.own_rows, m.other_rows = m.other_slope, m.other_active
+    gather = Gather(seat, m)
+    model = Layers(seat, m)
+    scatter = Scatter(seat, m, model.fill)
+
+    rows = m.total.shape[0]
+    pieces = [(m.inproj_two, 2 * m.block.shape[1], PIECE, 0, 0), (m.gain_rows, 0, PIECE, 0, 1)]
+    chunk = 1
+    for source, wide in (
+        (m.inproj_one, 3),
+        (m.outproj_one, 1),
+        (m.expand_one, 4),
+        (m.shrink_one, 4),
+        (m.inproj_two, 2),
+        (m.outproj_two, 1),
+        (m.expand_two, 4),
+        (m.shrink_two, 4),
+    ):
+        for j in range(wide):
+            pieces.append((source, j * CHUNK, CHUNK, chunk, 0))
+            chunk += 1
+    loads = []
+    for i, (source, start, size, chunk, side) in enumerate(pieces):
+        place = (slice(32 * (chunk // 4), 32 * (chunk // 4) + rows),)
+        place += (pl.ds(CHUNK * (chunk % 4) + PIECE * side, size),)
+        loads.append(
+            pltpu.make_async_copy(
+                source.at[:, pl.ds(start, size)], m.own_rows.at[place], m.load_sem.at[i]
+            )
+        )
+    m.block_load = pltpu.make_async_copy(m.block, m.mixed_grad, m.load_sem.at[CHUNKS + 1])
+    m.above_load = pltpu.make_async_copy(m.above, m.out_low.at[1], m.load_sem.at[CHUNKS + 2])
+    for load in loads + [m.block_load, m.above_load]:
+        load.start()
+    for i, load in enumerate(loads):
+        load.wait()
+        if i >= 1:
+            gather.swap(pieces[i][3], 1 - seat.core).start()
+
+    def tick(t):
+        when(t < CHUNKS + GATHER_LAGS[-1], lambda: gather.round(t))
+        chunk = t - GATHER_LAGS[-1]
+        when((chunk >= 0) & (chunk < CHUNKS), lambda: model.forward(chunk))
+        when(t == CHUNKS + GATHER_LAGS[-1] - 1, lambda: loop(CHUNKS, gather.drain))
+        model.backward(t)
+        turn = t - FIRST_TURN
+        for which, first in enumerate((4, 8, 12, 15, 19)):
+            when(turn == first, lambda which=which: seat.take(m.credit, which))
+        scatter.round(turn)
+        when(turn == 10, lambda: seat.signal(m.pair_credit.at[0], seat.partner))
+
+    loop(TICKS, tick)
+
+
+def run_layers(layers, block, segment, above, gain_rows, weights):
+    tokens, width = block.shape
+    rows, hidden = weights[2].shape[0], weights[2].shape[1]
+    low, wide = jnp.bfloat16, jnp.float32
+    names, args, in_specs = [], [], []
+    for name, value in (("block", block), ("segment", segment), ("above", above)):
+        names.append(name)
+        args.append(value)
+        space = pltpu.VMEM if name == "segment" else pl.ANY
+        in_specs.append(pl.BlockSpec(memory_space=space))
+    matrices = ("inproj", "outproj", "expand", "shrink")
+    for name, value in zip(
+        ["gain_rows"] + [n + end for end in ("_one", "_two") for n in matrices],
+        [gain_rows] + list(weights),
+    ):
+        names.append(name)
+        args.append(value)
+        in_specs.append(pl.BlockSpec(memory_space=pl.ANY))
+    outs = (
+        ("output", (tokens, width), wide),
+        ("grad", (tokens, width), wide),
+        ("total", (rows, CHUNKS * CHUNK), wide),
+    )
+    both = 2 * rows
+    scratch = (
+        ("held", (layers, 2, 2, both, REGIONS * CHUNK), low),
+        ("extra", (CHUNKS, both, PIECE), low),
+        ("extra_four", (CHUNKS // 4, 2, 2, both, PIECE), low),
+        ("extra_two", (CHUNKS // 4, 2, both, PIECE), low),
+        ("finished", (4, both, PIECE), wide),
+        ("gains", (8, width), wide),
+        ("gain_grads", (8, width), wide),
+        ("other_gain_grads", (8, width), wide),
+        ("allowed", (tokens, tokens), wide),
+        ("entered", (2, tokens, width), wide),
+        ("attn_in", (2, tokens, width), low),
+        ("proj", (2, tokens, 3 * width), low),
+        ("mixed", (2, tokens, width), low),
+        ("middle", (2, tokens, width), wide),
+        ("mlp_in", (2, tokens, width), low),
+        ("active", (2, tokens, hidden), low),
+        ("slope", (2, tokens, hidden), low),
+        ("out_low", (2, tokens, width), low),
+        ("branch", (2, tokens, width), low),
+        ("mixed_grad", (tokens, width), low),
+        ("carried", (tokens, width // 2), wide),
+        ("scratch", (tokens, width), wide),
+        ("other_out_low", (tokens, width), low),
+        ("other_active", (tokens, hidden), low),
+        ("other_mlp_in", (tokens, width), low),
+        ("other_slope", (tokens, hidden), low),
+        ("other_mixed", (tokens, width), low),
+        ("other_branch", (tokens, width), low),
+        ("other_attn_in", (2, tokens, width), low),
+        ("other_proj", (tokens, 3 * width), low),
+        ("other_fresh", (tokens, width // 2), low),
+    )
+    waits = (
+        ("load_sem", pltpu.SemaphoreType.DMA((CHUNKS + 3,))),
+        ("pre_sem", pltpu.SemaphoreType.DMA((2, CHUNKS))),
+        ("gather_recv", pltpu.SemaphoreType.DMA((CHUNKS, 7))),
+        ("gather_send", pltpu.SemaphoreType.DMA((CHUNKS, 11))),
+        ("scatter_recv", pltpu.SemaphoreType.DMA((CHUNKS, 8))),
+        ("scatter_send", pltpu.SemaphoreType.DMA((CHUNKS, 7))),
+        ("pair_sem", pltpu.SemaphoreType.DMA((2, 2, 11))),
+        ("credit", pltpu.SemaphoreType.REGULAR((5, 4))),
+        ("pair_credit", pltpu.SemaphoreType.REGULAR((1,))),
+    )
+    names += [n for n, _, _ in outs] + [n for n, _, _ in scratch] + [n for n, _ in waits]
+    return pl.pallas_call(
+        functools.partial(whole_kernel, layers, tuple(names)),
+        out_shape=[jax.ShapeDtypeStruct(shape, kind) for _, shape, kind in outs],
+        in_specs=in_specs,
+        out_specs=[pl.BlockSpec(memory_space=pltpu.VMEM)] * len(outs),
+        scratch_shapes=[pltpu.VMEM(shape, kind) for _, shape, kind in scratch]
+        + [kind for _, kind in waits],
+        compiler_params=pltpu.CompilerParams(
+            collective_id=0, has_side_effects=True, vmem_limit_bytes=67043328
+        ),
+    )(*args)
+
+
+def per_device_linked(
+    layers,
+    block_input,
+    segment_ids,
+    output_grad,
+    prenorm_one,
+    inproj_one,
+    outproj_one,
+    midnorm_one,
+    expand_one,
+    shrink_one,
+    prenorm_two,
+    inproj_two,
+    outproj_two,
+    midnorm_two,
+    expand_two,
+    shrink_two,
+):
+    width = block_input.shape[1]
+    hidden = expand_one.shape[1]
+    gains = jnp.stack([prenorm_one, midnorm_one, prenorm_two, midnorm_two], axis=1)
+    gain_rows = jnp.pad(gains, ((0, 0), (0, PIECE - 4)))
+    weights = (
+        inproj_one,
+        outproj_one.T,
+        expand_one,
+        shrink_one.T,
+        inproj_two,
+        outproj_two.T,
+        expand_two,
+        shrink_two.T,
+    )
+    output, grad, total = run_layers(
+        layers, block_input, segment_ids, output_grad, gain_rows, weights
+    )
+
+    def took(start, size):
+        return total[:, start : start + size]
+
+    def weights_of(base, proj):
+        return (
+            proj,
+            took(base, width).T,
+            took(base + width, hidden),
+            took(base + width + hidden, hidden).T,
+        )
+
+    one_grads = weights_of(CHUNK + 3 * width, took(CHUNK, 3 * width))
+    base = CHUNK + 4 * width + 2 * hidden
+    two_grads = weights_of(
+        base + 2 * width, jnp.concatenate([took(base, 2 * width), took(0, width // 2)], axis=1)
+    )
+    return (
+        output,
+        grad,
+        total[:, PIECE],
+        one_grads[0],
+        one_grads[1],
+        total[:, PIECE + 1],
+        one_grads[2],
+        one_grads[3],
+        total[:, PIECE + 2],
+        two_grads[0],
+        two_grads[1],
+        total[:, PIECE + 3],
+        two_grads[2],
+        two_grads[3],
+    )
+
+
 def solution(mesh):
+    layers = mesh.shape["dp"]
+    linked = layers == 4 and mesh.shape["fsdp"] == 8
+    step = functools.partial(per_device_linked, layers) if linked else per_device
     return jax.shard_map(
-        per_device,
+        step,
         mesh=mesh,
         in_specs=(
             P(("dp", "fsdp"), None),

time: 1330 us -> 300 us (0.23); the launches traced: 1310 us -> 300 us
  waiting for transfers between devices: 1020 us -> 0 us
  Pallas kernels: 0 us -> 286 us
  matrix products: 105 us -> 0 us
  local copies, waits for them, and re-layouts: 111 us -> 11.3 us
  blocking collectives: 42.3 us -> 0 us
  between operations: 15.6 us -> 0.67 us
    all_gather x8 -> x0, waiting for transfers between devices: 387 us -> none  [the longest x2 121 us: gather_weights(): lax.all_gather(expand, ('dp', 'fsdp'), axis=0, tiled=True)]
    unnamed x11 -> x0, waiting for transfers between devices: 379 us -> none
    pallas_call x0 -> x1, Pallas kernels: none -> 286 us  [run_layers(): pl.pallas_call(functools.partial(whole_kernel, layers, tuple(names)), out...]
    reduce_scatter x1 -> x0, waiting for transfers between devices: 259 us -> none  [sum_grads(): lax.psum_scatter(jnp.concatenate([rows_product(attn_in, proj_grad), rows_...]
    dot_general x36 -> x0, matrix products: 105 us -> none  [the longest x8 32.6 us: rows_product(): lax.dot_general(left, right, (((0,), (0,)), ((), ())), preferred_element_...]
    concatenate x3 -> x0, local copies, waits for them, and re-layouts: 63.5 us -> none  [the longest x2 61.5 us: sum_grads(): jnp.concatenate([rows_product(attn_in, proj_grad), rows_product(branch_lo...]
    unnamed x1 -> x0, blocking collectives: 42.3 us -> none
    unnamed x222 -> x6, local copies, waits for them, and re-layouts: 17.6 us -> 1.77 us
  transfers between devices with their start and end apart: 10 -> 0, of which waited for: 10 -> 0; matrix products, arithmetic and copies ran while one was open for 9% -> 0% of each run, Pallas kernels for 0% -> 0%
where the time goes in v2:
time: 300 us
  Pallas kernels  286 us (95%)
  local copies, waits for them, and re-layouts  11.3 us (4%)
    pallas_call x1, Pallas kernels, run_layers(): pl.pallas_call(functools.partial(whole_kernel, layers, tuple(names)), out...  286 us

profile of v2, /device:TPU:0, one launch (start us, length us, event | category | flops | bytes accessed | tf_op | source)
XLA Modules:
  0.0 299.8 jit_solution(7963786351917605585)
XLA Ops:
  0.6 0.7 pad_maximum_fusion.1
  1.4 0.1 copy.37
  1.5 0.6 pad.4.refs_3_
  2.1 286.4 %shard_map.254 = (f32[256,768]{1,0:T(8,128)}, f32[256,768]{1,0:T(8,128)}, f32[24,18432]{1,0:T(8,128)}) custom-call(bf16[256,768]{1,0:T(8,128)(2,1)} %refs_0_.1, s32[1,256]{1,0:T(1,128)} %refs_1_.1, bf16[256,768]{1,0:T(8,128)(2,1)} %refs_2_.1, bf16[24,384]{1,0:T(8,128)(2,1)} %pad.4.refs_3_, bf16[24,2304]{1,0:T(8,128)(2,1)} %refs_4_.1, ...), custom_call_target="tpu_custom_call" | custom-call | tf_op jit(solution)/shard_map/pallas_call | solution.py:1345
  288.5 1.6 slice_reduce_fusion
  290.1 0.8 slice.47
  290.8 0.9 slice.46
  291.7 0.0 copy-start.1
  291.8 0.7 pad_maximum_fusion
  292.4 1.6 slice_bitcast_fusion.2
  294.0 1.6 slice.40
  295.7 0.0 copy-start
  295.7 2.3 slice_bitcast_fusion
  298.0 0.0 copy-done.1
  298.0 0.9 copy.40
  298.9 0.0 copy-done
  298.9 0.9 copy.41
Async XLA Ops:
  291.7 6.2 %copy-start.1 = (f32[256,768]{1,0:T(8,128)S(1)}, f32[256,768]{1,0:T(8,128)}, u32[]{:S(2)}) copy-start(f32[256,768]{1,0:T(8,128)} %get-tuple-element.44) | copy-start | bytes 2359300
  295.7 3.2 %copy-start = (f32[256,768]{1,0:T(8,128)S(1)}, f32[256,768]{1,0:T(8,128)}, u32[]{:S(2)}) copy-start(f32[256,768]{1,0:T(8,128)} %get-tuple-element.45) | copy-start | bytes 2359300
